TPU v7x, 512 devices: a whole 4x8x8 slice. The times are simulated.
512 devices in a mesh: chan: 64 (over z, y_lo, x), facet: 8 (over y_hi, core).
Axes of the slice: x: 4, y: 8 (y_hi: 4, y_lo: 2; y = y_hi * 2 + y_lo), z: 8, core: 2. Of those that a mesh axis runs over, the one named last changes fastest.
Arguments:
- estimate: float32 [256, 128, 1024], P('chan', None, 'facet'), may hold values from -16 to 16
- dirty: float32 [256, 128, 1024], P('chan', None, 'facet'), may hold values from -16 to 16
- weights: float32 [256, 128, 1024], P('chan', None, 'facet'), may hold values from 0.2 to 1
- margin: int32 [8], replicated, may hold values from 1 to 16, as said below
- blend_table: int32 [8, 160], replicated, may hold values from 1 to 8
- tau_steps: int32 [2], replicated, may hold values from 1 to 4
Outputs:
- updated: float32 [256, 128, 1024], P('chan', None, 'facet')
Inputs may be any that keep to these rules, and one draw needn't show every extreme that they name: Some facet has margin exactly 16.
All inputs are finite; a program needn't handle non-finite values.
Results may differ from a plain program's by a relative error of at most 0.00012.
Values sent between devices are 32-bit elements; how exact they have to be, the bound alone decides.
No kernel may reach another device: no remote copies, remote signals or barrier semaphores. Data moves between devices by JAX's collectives and lax.ppermute only.
A program may use at most 64 MiB of HBM per device.

v0:
```python
import math

import jax
import jax.numpy as jnp
from jax import lax
from jax.sharding import PartitionSpec as P

OV = 16
NS_STEPS = 2
ITERS = 2


def padded(shard, sides, width):
    for axis, dim in sides:
        size, length = (lax.axis_size(axis), shard.shape[dim])
        up = [(i, (i + 1) % size) for i in range(size - 1)]
        down = [(j, i) for i, j in up]
        last = lax.slice_in_dim(shard, length - width, length, axis=dim)
        initial = lax.slice_in_dim(shard, 0, width, axis=dim)
        before = lax.ppermute(last, axis, up)
        after = lax.ppermute(initial, axis, down)
        shard = jnp.concatenate([before, shard, after], axis=dim)
    return shard


def apply_shrink(gram, columns, tau_value):
    channel_count = gram.shape[0]
    identity = jnp.eye(channel_count, dtype=jnp.float32)
    mean_eigen = jnp.trace(gram) / channel_count + 1e-06
    target = (gram + 0.01 * mean_eigen * identity) / (16.16 * mean_eigen)
    inverse_root = identity
    for newton_step in range(NS_STEPS):
        middle = 1.5 * identity - 0.5 * jnp.dot(
            inverse_root, target, precision=lax.Precision.HIGHEST
        )
        target = jnp.dot(target, middle, precision=lax.Precision.HIGHEST)
        inverse_root = jnp.dot(middle, inverse_root, precision=lax.Precision.HIGHEST)
    factor = 0.1 * tau_value / math.sqrt(1.01)
    kernel = identity - factor * inverse_root
    return jnp.dot(kernel, columns, precision=lax.Precision.HIGHEST)


def shrink_block(block, tau_value):
    columns = block.reshape(block.shape[0], -1)
    partial_value = jnp.dot(columns, columns.T, precision=lax.Precision.HIGHEST)
    gram = lax.psum(partial_value, "chan")
    return apply_shrink(gram, columns, tau_value).reshape(block.shape)


def extend(moved_cube):
    return padded(moved_cube, (("facet", 2),), OV)


def blend_sums(margin, blend_table, facet_id, facet_total, center):
    center_index = jnp.arange(center, dtype=jnp.int32)
    table_float = blend_table.astype(jnp.float32)
    own_part = table_float[facet_id][OV : OV + center]
    before_id = jnp.maximum(facet_id - 1, 0)
    after_id = jnp.minimum(facet_id + 1, facet_total - 1)
    before_slice = jnp.pad(table_float[before_id][center + OV :], (0, center - OV))
    after_slice = jnp.pad(table_float[after_id][:OV], (center - OV, 0))
    before_ok = (facet_id > 0) & (center_index < margin[before_id])
    after_ok = (facet_id < facet_total - 1) & (center_index >= center - margin[after_id])
    return (
        own_part + jnp.where(before_ok, before_slice, 0.0) + jnp.where(after_ok, after_slice, 0.0)
    )


def blend(result, row_weight, denominator, center):
    weighted = result * row_weight
    rims = jnp.concatenate([weighted[:, :, :OV], weighted[:, :, center + OV :]], axis=2)
    received = padded(rims, (("facet", 2),), OV)
    from_before = jnp.pad(received[:, :, :OV], ((0, 0), (0, 0), (0, center - OV)))
    from_after = jnp.pad(
        received[:, :, received.shape[2] - OV :], ((0, 0), (0, 0), (center - OV, 0))
    )
    core_rows = weighted[:, :, OV : OV + center] + from_before + from_after
    return core_rows / denominator


def per_device(estimate, dirty, weights, margin, blend_table, tau_steps):
    facet_id = lax.axis_index("facet")
    facet_total = lax.axis_size("facet")
    center = estimate.shape[2]
    ext_len = center + 2 * OV
    row_index = jnp.arange(ext_len, dtype=jnp.int32)
    own_width = margin[facet_id]
    keep_rows = ((row_index >= OV - own_width) & (row_index < center + OV + own_width)).astype(
        jnp.float32
    )
    row_weight = blend_table[facet_id].astype(jnp.float32) * keep_rows
    denominator = blend_sums(margin, blend_table, facet_id, facet_total, center)
    current = estimate
    for iteration in range(ITERS):
        tau_value = tau_steps[iteration].astype(jnp.float32)
        moved_cube = current - weights * (current - dirty)
        extended = extend(moved_cube) * keep_rows
        pixel_view = lax.all_to_all(extended, "chan", split_axis=1, concat_axis=0, tiled=True)
        result = shrink_block(pixel_view, tau_value)
        back_view = lax.all_to_all(result, "chan", split_axis=0, concat_axis=1, tiled=True)
        current = blend(back_view, row_weight, denominator, center)
    return current


def solution(mesh):
    placed = (
        P("chan", None, "facet"),
        P("chan", None, "facet"),
        P("chan", None, "facet"),
        P(),
        P(),
        P(),
    )
    return jax.shard_map(
        per_device, mesh=mesh, in_specs=placed, out_specs=P("chan", None, "facet"), check_vma=False
    )
```

profile of v0, /device:TPU:1, one launch (start us, length us, event | category | flops | bytes accessed | tf_op | source)
XLA Modules:
  0.0 1311.3 jit_solution(14268849020404267029)
XLA Ops:
  6.5 1.1 multiply_subtract_fusion.1
  7.8 5.6 collective-permute-start
  13.4 4.5 collective-permute-start.1
  17.9 0.6 copy-done.5
  18.6 0.7 fusion.28
  20.5 4.3 collective-permute-done.1
  25.4 26.8 %all_to_all.66 = f32[4,128,160]{2,0,1:T(4,128)S(1)} all-to-all(f32[4,128,160]{2,0,1:T(4,128)S(1)} %copy.53), channel_id=1, replica_groups=mesh['chan'=64,'facet'=8] {'chan'}, dimensions={1} | all-to-all | bytes 655360 | tf_op jit(solution)/shard_map/all_to_all | solution.py:98
  53.0 1.3 fusion.29
  56.3 531.9 %all-reduce.9.cloned.1.call-done = f32[256,256]{1,0:T(8,128)} async-done(((f32[256,256]{1,0:T(8,128)}), f32[256,256]{1,0:T(8,128)}) %all-reduce.9.cloned.1.call-update) | async-done | bytes 262160 | tf_op jit(solution)/shard_map/psum | solution.py:46
  588.3 1.7 select_reduce_fusion.1
  592.9 1.0 copy.56
  593.9 9.1 all-to-all-start.1
  604.5 11.8 all-to-all-done.1
  616.7 35.2 %collective-permute-start.2 = (f32[4,128,16]{2,1,0:T(8,128)S(1)}, f32[4,128,16]{2,1,0:T(8,128)S(1)}, u32[]{:S(2)}, u32[]{:S(2)}) collective-permute-start(f32[4,128,16]{2,1,0:T(8,128)S(1)} %get-tuple-element.7), channel_id=1, source_target_pairs={{0,1},{1,2},{2,3},{3,4},{4,5},{5,6},{6,7},{8,9},{9,10},{10,11},{11... | collective-permute-start | bytes 98312 | tf_op jit(solution)/shard_map/ppermute | solution.py:20
  651.9 1.9 collective-permute-start.3
  653.8 0.7 fusion.17
  654.5 0.7 collective-permute-done.2
  655.2 8.1 collective-permute-done.3
  663.6 1.9 collective-permute-start.4
  665.6 2.4 collective-permute-start.5
  668.0 0.9 collective-permute-done.4
  668.9 7.9 collective-permute-done.5
  677.5 18.4 %all_to_all.67 = f32[4,128,160]{2,0,1:T(4,128)S(1)} all-to-all(f32[4,128,160]{2,0,1:T(4,128)S(1)} %copy.59), channel_id=1, replica_groups=mesh['chan'=64,'facet'=8] {'chan'}, dimensions={1} | all-to-all | bytes 655360 | tf_op jit(solution)/shard_map/all_to_all | solution.py:98
  696.6 1.3 fusion.31
  698.7 530.9 %all-reduce.11.cloned.1.call-done = f32[256,256]{1,0:T(8,128)} async-done(((f32[256,256]{1,0:T(8,128)}), f32[256,256]{1,0:T(8,128)}) %all-reduce.11.cloned.1.call-update) | async-done | bytes 262160 | tf_op jit(solution)/shard_map/psum | solution.py:46
  1229.6 1.7 select_reduce_fusion
  1234.4 22.2 %all_to_all.68 = f32[256,2,160]{2,1,0:T(2,128)S(1)} all-to-all(f32[256,2,160]{2,1,0:T(2,128)S(1)} %copy.62), channel_id=1, replica_groups=mesh['chan'=64,'facet'=8] {'chan'}, dimensions={0} | all-to-all | bytes 655360 | tf_op jit(solution)/shard_map/all_to_all | solution.py:100
  1257.0 35.2 %collective-permute-start.6 = (f32[4,128,16]{2,1,0:T(8,128)S(1)}, f32[4,128,16]{2,1,0:T(8,128)S(1)}, u32[]{:S(2)}, u32[]{:S(2)}) collective-permute-start(f32[4,128,16]{2,1,0:T(8,128)S(1)} %get-tuple-element.5), channel_id=1, source_target_pairs={{0,1},{1,2},{2,3},{3,4},{4,5},{5,6},{6,7},{8,9},{9,10},{10,11},{11... | collective-permute-start | bytes 98312 | tf_op jit(solution)/shard_map/ppermute | solution.py:20
  1292.2 1.9 collective-permute-start.7
  1294.1 1.4 collective-permute-done.6
  1295.5 8.1 collective-permute-done.7
  1303.6 0.9 fusion.9
  (56 shorter events, 10.9 us)
Async XLA Ops:
  6.5 581.7 %all-reduce.9.cloned.1.call-start = ((), (), s32[]{:S(2)}) async-start(), calls=%async_computation.4 | async-start | bytes 524288 | tf_op jit(solution)/shard_map/psum | solution.py:46
  7.8 12.7 collective-permute-start
  13.4 11.4 collective-permute-start.1
  17.9 0.7 copy-start.5
  54.3 0.7 copy-start.6
  588.3 2.3 copy-start.3
  593.9 22.4 %all-to-all-start.1 = ((f32[256,2,160]{2,1,0:T(2,128)}), f32[256,2,160]{2,1,0:T(2,128)S(1)}, u32[]{:S(2)}, u32[]{:S(2)}) async-start(f32[256,2,160]{2,1,0:T(2,128)} %copy.56), calls=%async_computation.1 | async-start | bytes 1048576 | tf_op jit(solution)/shard_map/all_to_all | solution.py:100
  603.1 0.7 copy-start.4
  603.1 626.5 %all-reduce.11.cloned.1.call-start = ((), (), s32[]{:S(2)}) async-start(), calls=%async_computation.5 | async-start | bytes 524288 | tf_op jit(solution)/shard_map/psum | solution.py:46
  616.6 46.7 %copy-start = (f32[4,128,128]{2,1,0:T(8,128)S(1)}, f32[4,128,128]{2,1,0:T(8,128)}, u32[]{:S(2)}) copy-start(f32[4,128,128]{2,1,0:T(8,128)} %param.8) | copy-start | bytes 786436
  616.6 46.7 %copy-start.1 = (f32[4,128,128]{2,1,0:T(8,128)S(1)}, f32[4,128,128]{2,1,0:T(8,128)}, u32[]{:S(2)}) copy-start(f32[4,128,128]{2,1,0:T(8,128)} %param.7) | copy-start | bytes 786436
  616.7 38.5 %collective-permute-start.2 = (f32[4,128,16]{2,1,0:T(8,128)S(1)}, f32[4,128,16]{2,1,0:T(8,128)S(1)}, u32[]{:S(2)}, u32[]{:S(2)}) collective-permute-start(f32[4,128,16]{2,1,0:T(8,128)S(1)} %get-tuple-element.7), channel_id=1, source_target_pairs={{0,1},{1,2},{2,3},{3,4},{4,5},{5,6},{6,7},{8,9},{9,10},{10,11},{11... | collective-permute-start | bytes 98312 | tf_op jit(solution)/shard_map/ppermute | solution.py:20
  651.9 11.4 collective-permute-start.3
  663.6 5.3 collective-permute-start.4
  665.6 11.3 collective-permute-start.5
  1229.6 2.3 copy-start.2
  1257.0 38.5 %collective-permute-start.6 = (f32[4,128,16]{2,1,0:T(8,128)S(1)}, f32[4,128,16]{2,1,0:T(8,128)S(1)}, u32[]{:S(2)}, u32[]{:S(2)}) collective-permute-start(f32[4,128,16]{2,1,0:T(8,128)S(1)} %get-tuple-element.5), channel_id=1, source_target_pairs={{0,1},{1,2},{2,3},{3,4},{4,5},{5,6},{6,7},{8,9},{9,10},{10,11},{11... | collective-permute-start | bytes 98312 | tf_op jit(solution)/shard_map/ppermute | solution.py:20
  1292.2 11.4 collective-permute-start.7
Sparse Core Ops, SparseCore 0:
  54.4 533.8 all-reduce.8
  698.1 531.4 all-reduce.10
where the time goes:
time: 1310 us
  waiting for transfers between devices  1110 us (85%)
  starting transfers between devices  97.7 us (7%)
  blocking collectives  67.4 us (5%)
  between operations  18.3 us (1%)
    psum x2, waiting for transfers between devices, shrink_block(): gram = lax.psum(partial_value, 'chan')  1060 us
    ppermute x4, starting transfers between devices, padded(): before = lax.ppermute(last, axis, up)  77.8 us
    all_to_all x2, blocking collectives, per_device(): lax.all_to_all(extended, 'chan', split_axis=1, concat_axis=0, tiled=True)  45.2 us
    ppermute x4, waiting for transfers between devices, padded(): after = lax.ppermute(initial, axis, down)  28.3 us
  transfers between devices with their start and end apart: 11, of which 10 were waited for; matrix products, arithmetic and copies ran while one was open for 0% of the time, Pallas kernels for 0%

commit v1 on v0

v1 whole, which is shorter than its diff:
```python
import math

import jax
import jax.numpy as jnp
from jax import lax
from jax.sharding import PartitionSpec as P

OV = 16
NS_STEPS = 2
ITERS = 2
HI = lax.Precision.HIGHEST


def to_pixels(stack, n):
    a, cl, w, hd = stack.shape
    wl = w // n
    sent = stack.reshape(a, cl, n, wl, hd).transpose(2, 0, 1, 3, 4).reshape(n, a * cl * wl, hd)
    got = lax.all_to_all(sent, "chan", 0, 0)
    return got.reshape(n, a, cl, wl, hd).transpose(1, 0, 2, 3, 4).reshape(a, n * cl, wl, hd)


def to_channels(pix, n):
    c, wl, hd = pix.shape
    cl = c // n
    got = lax.all_to_all(pix.reshape(n, cl * wl, hd), "chan", 0, 0)
    return got.reshape(n, cl, wl, hd).transpose(1, 0, 2, 3).reshape(cl, n * wl, hd)


def swap(low, high):
    size = lax.axis_size("facet")
    up = [(i, i + 1) for i in range(size - 1)]
    down = [(i + 1, i) for i in range(size - 1)]
    shape = low.shape

    def move(x, pairs):
        return lax.ppermute(x.reshape(-1, 128), "facet", pairs).reshape(shape)

    return move(high, up), move(low, down)


def total_gram(partial, n):
    c = partial.shape[0]
    tiles = partial.reshape(c // 8, 8, c // 128, 128).transpose(0, 2, 1, 3).reshape(n, -1, 128)
    mine = jnp.sum(lax.all_to_all(tiles, "chan", 0, 0), axis=0)
    every = lax.all_to_all(jnp.broadcast_to(mine[None], tiles.shape), "chan", 0, 0)
    return every.reshape(c // 8, c // 128, 8, 128).transpose(0, 2, 1, 3).reshape(c, c)


def shrink_kernel(gram, tau_value):
    channel_count = gram.shape[0]
    identity = jnp.eye(channel_count, dtype=jnp.float32)
    mean_eigen = jnp.trace(gram) / channel_count + 1e-06
    target = (gram + 0.01 * mean_eigen * identity) / (16.16 * mean_eigen)
    inverse_root = identity
    for newton_step in range(NS_STEPS):
        middle = 1.5 * identity - 0.5 * jnp.dot(inverse_root, target, precision=HI)
        if newton_step + 1 < NS_STEPS:
            target = jnp.dot(target, middle, precision=HI)
        inverse_root = jnp.dot(middle, inverse_root, precision=HI)
    factor = 0.1 * tau_value / math.sqrt(1.01)
    return identity - factor * inverse_root


def per_device(estimate, dirty, weights, margin, blend_table, tau_steps):
    n = lax.axis_size("chan")
    facet_id = lax.axis_index("facet")
    facet_total = lax.axis_size("facet")
    center = estimate.shape[2]
    ext_len = center + 2 * OV
    row_index = jnp.arange(ext_len, dtype=jnp.int32)[None, :]
    keep_all = (
        (row_index >= OV - margin[:, None]) & (row_index < center + OV + margin[:, None])
    ).astype(jnp.float32)
    weight_all = blend_table.astype(jnp.float32) * keep_all
    keep_rows = keep_all[facet_id]
    row_weight = weight_all[facet_id]
    before = weight_all[jnp.maximum(facet_id - 1, 0)][center:] * (facet_id > 0)
    after = weight_all[jnp.minimum(facet_id + 1, facet_total - 1)][: 2 * OV] * (
        facet_id < facet_total - 1
    )
    denominator = row_weight + jnp.concatenate(
        [before, jnp.zeros((center - 2 * OV,), jnp.float32), after]
    )
    denominator = jnp.where(denominator == 0.0, 1.0, denominator)

    moved = estimate - weights * (estimate - dirty)
    stack = to_pixels(jnp.stack([moved, dirty, weights]), n)
    from_before, from_after = swap(stack[..., :OV], stack[..., center - OV :])
    stack = jnp.concatenate([from_before, stack, from_after], axis=-1)
    moved, dirty, weights = stack[0], stack[1], stack[2]
    for iteration in range(ITERS):
        tau_value = tau_steps[iteration].astype(jnp.float32)
        block = moved * keep_rows
        columns = block.reshape(block.shape[0], -1)
        gram = total_gram(jnp.dot(columns, columns.T, precision=HI), n)
        shrunk = jnp.dot(shrink_kernel(gram, tau_value), columns, precision=HI).reshape(block.shape)
        weighted = shrunk * row_weight
        last = iteration + 1 == ITERS
        if last:
            from_before, from_after = swap(weighted[..., :OV], weighted[..., center + OV :])
            middle = weighted[..., OV : OV + center]
            gap = jnp.zeros(middle.shape[:-1] + (center - 2 * OV,), jnp.float32)
            middle = middle + jnp.concatenate([from_before, gap, from_after], axis=-1)
            current = middle / denominator[OV : OV + center]
        else:
            from_before, from_after = swap(weighted[..., : 2 * OV], weighted[..., center:])
            gap = jnp.zeros(weighted.shape[:-1] + (center - 2 * OV,), jnp.float32)
            current = weighted + jnp.concatenate([from_before, gap, from_after], axis=-1)
            current = current / denominator
            moved = current - weights * (current - dirty)
    return to_channels(current, n)


def solution(mesh):
    placed = (
        P("chan", None, "facet"),
        P("chan", None, "facet"),
        P("chan", None, "facet"),
        P(),
        P(),
        P(),
    )
    return jax.shard_map(
        per_device, mesh=mesh, in_specs=placed, out_specs=P("chan", None, "facet"), check_vma=False
    )
```

time: 1310 us -> 180 us (0.14)
  waiting for transfers between devices: 1110 us -> 54.5 us
  starting transfers between devices: 97.7 us -> 60.3 us
  blocking collectives: 67.4 us -> 30.5 us
  between operations: 18.3 us -> 3.11 us
    psum x2 -> x0, waiting for transfers between devices: 1060 us -> none  [shrink_block(): gram = lax.psum(partial_value, 'chan')]
    ppermute x8 -> x6, starting transfers between devices: 88.6 us -> 28.9 us  [move(): return lax.ppermute(x.reshape(-1, 128), 'facet', pairs).reshape(shape)]
    all_to_all x1 -> x4, waiting for transfers between devices: 11.8 us -> 53 us  [the longest x1 21.4 us: to_pixels(): got = lax.all_to_all(sent, 'chan', 0, 0)]
    all_to_all x3 -> x2, blocking collectives: 67.4 us -> 30.5 us  [the longest x1 15.5 us: total_gram(): mine = jnp.sum(lax.all_to_all(tiles, 'chan', 0, 0), axis=0)]
    ppermute x8 -> x6, waiting for transfers between devices: 31.4 us -> 1.49 us  [move(): return lax.ppermute(x.reshape(-1, 128), 'facet', pairs).reshape(shape)]
    all_to_all x1 -> x4, starting transfers between devices: 9.14 us -> 31.4 us  [the longest x1 15.3 us: to_pixels(): got = lax.all_to_all(sent, 'chan', 0, 0)]
  transfers between devices with their start and end apart: 11 -> 10, of which waited for: 10 -> 6; matrix products, arithmetic and copies ran while one was open for 0% -> 3% of each run, Pallas kernels for 0% -> 0%
where the time goes in v1:
time: 180 us; the launch traced here: 177 us
  starting transfers between devices  60.3 us (34%)
  waiting for transfers between devices  54.5 us (30%)
  blocking collectives  30.5 us (17%)
  local copies, waits for them, and re-layouts  18.1 us (10%)
  matrix products  6.34 us (4%)
  other arithmetic  4.04 us (2%)
  between operations  3.11 us (2%)
    ppermute x6, starting transfers between devices, move(): return lax.ppermute(x.reshape(-1, 128), 'facet', pairs).reshape(shape)  28.9 us
    all_to_all x1, waiting for transfers between devices, to_pixels(): got = lax.all_to_all(sent, 'chan', 0, 0)  21.4 us
    all_to_all x2, waiting for transfers between devices, total_gram(): lax.all_to_all(jnp.broadcast_to(mine[None], tiles.shape), 'chan', 0, 0)  21.3 us
    all_to_all x1, blocking collectives, total_gram(): mine = jnp.sum(lax.all_to_all(tiles, 'chan', 0, 0), axis=0)  15.5 us
    all_to_all x1, starting transfers between devices, to_pixels(): got = lax.all_to_all(sent, 'chan', 0, 0)  15.3 us
    all_to_all x1, blocking collectives, to_channels(): got = lax.all_to_all(pix.reshape(n, cl * wl, hd), 'chan', 0, 0)  15 us
    all_to_all x1, waiting for transfers between devices, total_gram(): mine = jnp.sum(lax.all_to_all(tiles, 'chan', 0, 0), axis=0)  10.3 us
    all_to_all x2, starting transfers between devices, total_gram(): lax.all_to_all(jnp.broadcast_to(mine[None], tiles.shape), 'chan', 0, 0)  9.43 us
  transfers between devices with their start and end apart: 10, of which 6 were waited for; matrix products, arithmetic and copies ran while one was open for 3% of the time, Pallas kernels for 0%

profile of v1, /device:TPU:1, one launch (start us, length us, event | category | flops | bytes accessed | tf_op | source)
XLA Modules:
  0.0 176.8 jit_solution(1638518238134586955)
XLA Ops:
  0.0 1.2 multiply_subtract_fusion
  1.7 1.4 copy.54
  3.1 15.3 %all-to-all-start = ((f32[64,24,128]{2,1,0:T(8,128)}), f32[64,24,128]{2,1,0:T(8,128)S(1)}, u32[]{:S(2)}, u32[]{:S(2)}) async-start(f32[64,24,128]{2,1,0:T(8,128)} %copy.54), calls=%async_computation | async-start | bytes 1572864 | tf_op jit(solution)/shard_map/all_to_all | solution.py:18
  18.5 0.6 copy-done.4
  19.2 21.4 %all-to-all-done = f32[64,24,128]{2,1,0:T(8,128)S(1)} async-done(((f32[64,24,128]{2,1,0:T(8,128)}), f32[64,24,128]{2,1,0:T(8,128)S(1)}, u32[]{:S(2)}, u32[]{:S(2)}) %all-to-all-start) | async-done | bytes 786464 | tf_op jit(solution)/shard_map/all_to_all | solution.py:18
  42.2 0.9 reshape.196
  43.1 4.0 %collective-permute-start.1 = (f32[192,128]{1,0:T(8,128)S(1)}, f32[192,128]{1,0:T(8,128)S(1)}, u32[]{:S(2)}, u32[]{:S(2)}) collective-permute-start(f32[192,128]{1,0:T(8,128)S(1)} %reshape.196), channel_id=1, source_target_pairs={{1,0},{2,1},{3,2},{4,3},{5,4},{6,5},{7,6},{9,8},{10,9},{11,10},{12... | collective-permute-start | bytes 294920 | tf_op jit(solution)/shard_map/ppermute | solution.py:36
  47.7 0.9 reshape.194
  48.6 4.1 %collective-permute-start = (f32[192,128]{1,0:T(8,128)S(1)}, f32[192,128]{1,0:T(8,128)S(1)}, u32[]{:S(2)}, u32[]{:S(2)}) collective-permute-start(f32[192,128]{1,0:T(8,128)S(1)} %reshape.194), channel_id=1, source_target_pairs={{0,1},{1,2},{2,3},{3,4},{4,5},{5,6},{6,7},{8,9},{9,10},{10,11},{11... | collective-permute-start | bytes 294920 | tf_op jit(solution)/shard_map/ppermute | solution.py:36
  53.0 1.0 reshape.197
  54.4 1.0 reshape.195
  56.8 1.3 fusion.10
  58.1 6.6 %all-to-all-start.1 = ((f32[64,8,128]{2,1,0:T(8,128)}), f32[64,8,128]{2,1,0:T(8,128)S(1)}, u32[]{:S(2)}, u32[]{:S(2)}) async-start(f32[64,8,128]{2,1,0:T(8,128)} %bitcast.14), calls=%async_computation.1 | async-start | bytes 524288 | tf_op jit(solution)/shard_map/all_to_all | solution.py:44
  64.7 0.6 copy-done.3
  66.1 10.3 %all-to-all-done.1 = f32[64,8,128]{2,1,0:T(8,128)S(1)} async-done(((f32[64,8,128]{2,1,0:T(8,128)}), f32[64,8,128]{2,1,0:T(8,128)S(1)}, u32[]{:S(2)}, u32[]{:S(2)}) %all-to-all-start.1) | async-done | bytes 262176 | tf_op jit(solution)/shard_map/all_to_all | solution.py:44
  76.5 0.7 broadcast_in_dim.15
  77.2 4.8 %all-to-all-start.2 = ((f32[64,8,128]{2,1,0:T(8,128)}), f32[64,8,128]{2,1,0:T(8,128)S(1)}, u32[]{:S(2)}, u32[]{:S(2)}) async-start(f32[64,8,128]{2,1,0:T(8,128)} %broadcast_in_dim.15), calls=%async_computation.2 | async-start | bytes 524288 | tf_op jit(solution)/shard_map/all_to_all | solution.py:45
  82.9 10.2 %all-to-all-done.2 = f32[64,8,128]{2,1,0:T(8,128)S(1)} async-done(((f32[64,8,128]{2,1,0:T(8,128)}), f32[64,8,128]{2,1,0:T(8,128)S(1)}, u32[]{:S(2)}, u32[]{:S(2)}) %all-to-all-start.2) | async-done | bytes 262176 | tf_op jit(solution)/shard_map/all_to_all | solution.py:45
  93.2 0.7 fusion.22
  97.2 4.7 %collective-permute-start.3 = (f32[128,128]{1,0:T(8,128)S(1)}, f32[128,128]{1,0:T(8,128)S(1)}, u32[]{:S(2)}, u32[]{:S(2)}) collective-permute-start(f32[128,128]{1,0:T(8,128)S(1)} %reshape.203), channel_id=1, source_target_pairs={{1,0},{2,1},{3,2},{4,3},{5,4},{6,5},{7,6},{9,8},{10,9},{11,10},{12... | collective-permute-start | bytes 196616 | tf_op jit(solution)/shard_map/ppermute | solution.py:36
  102.4 5.4 %collective-permute-start.2 = (f32[128,128]{1,0:T(8,128)S(1)}, f32[128,128]{1,0:T(8,128)S(1)}, u32[]{:S(2)}, u32[]{:S(2)}) collective-permute-start(f32[128,128]{1,0:T(8,128)S(1)} %reshape.201), channel_id=1, source_target_pairs={{0,1},{1,2},{2,3},{3,4},{4,5},{5,6},{6,7},{8,9},{9,10},{10,11},{11... | collective-permute-start | bytes 196616 | tf_op jit(solution)/shard_map/ppermute | solution.py:36
  108.2 0.9 collective-permute-done.2
  111.0 15.5 %all_to_all.30 = f32[64,8,128]{2,1,0:T(8,128)S(1)} all-to-all(f32[64,8,128]{2,1,0:T(8,128)S(1)} %bitcast.115), channel_id=1, replica_groups=mesh['chan'=64,'facet'=8] {'chan'}, dimensions={0} | all-to-all | bytes 524288 | tf_op jit(solution)/shard_map/all_to_all | solution.py:44
  126.6 0.7 broadcast_in_dim.33
  127.3 4.6 %all-to-all-start.4 = ((f32[64,8,128]{2,1,0:T(8,128)}), f32[64,8,128]{2,1,0:T(8,128)S(1)}, u32[]{:S(2)}, u32[]{:S(2)}) async-start(f32[64,8,128]{2,1,0:T(8,128)} %broadcast_in_dim.33), calls=%async_computation.4 | async-start | bytes 524288 | tf_op jit(solution)/shard_map/all_to_all | solution.py:45
  132.6 11.0 %all-to-all-done.4 = f32[64,8,128]{2,1,0:T(8,128)S(1)} async-done(((f32[64,8,128]{2,1,0:T(8,128)}), f32[64,8,128]{2,1,0:T(8,128)S(1)}, u32[]{:S(2)}, u32[]{:S(2)}) %all-to-all-start.4) | async-done | bytes 262176 | tf_op jit(solution)/shard_map/all_to_all | solution.py:45
  143.6 0.7 fusion.23
  147.8 1.9 %collective-permute-start.5 = (f32[64,128]{1,0:T(8,128)S(1)}, f32[64,128]{1,0:T(8,128)S(1)}, u32[]{:S(2)}, u32[]{:S(2)}) collective-permute-start(f32[64,128]{1,0:T(8,128)S(1)} %reshape.211), channel_id=1, source_target_pairs={{1,0},{2,1},{3,2},{4,3},{5,4},{6,5},{7,6},{9,8},{10,9},{11,10},{12... | collective-permute-start | bytes 98312 | tf_op jit(solution)/shard_map/ppermute | solution.py:36
  150.1 8.8 %collective-permute-start.4 = (f32[64,128]{1,0:T(8,128)S(1)}, f32[64,128]{1,0:T(8,128)S(1)}, u32[]{:S(2)}, u32[]{:S(2)}) collective-permute-start(f32[64,128]{1,0:T(8,128)S(1)} %reshape.209), channel_id=1, source_target_pairs={{0,1},{1,2},{2,3},{3,4},{4,5},{5,6},{6,7},{8,9},{9,10},{10,11},{11... | collective-permute-start | bytes 98312 | tf_op jit(solution)/shard_map/ppermute | solution.py:36
  159.5 0.6 collective-permute-done.4
  160.9 15.0 %all_to_all.31 = f32[64,8,128]{2,1,0:T(8,128)S(1)} all-to-all(f32[64,8,128]{2,1,0:T(8,128)S(1)} %bitcast.113), channel_id=1, replica_groups=mesh['chan'=64,'facet'=8] {'chan'}, dimensions={0} | all-to-all | bytes 524288 | tf_op jit(solution)/shard_map/all_to_all | solution.py:25
  175.9 0.9 copy.76
  (83 shorter events, 15.6 us)
Async XLA Ops:
  0.0 1.2 copy-start
  0.0 1.3 copy-start.1
  3.1 37.5 %all-to-all-start = ((f32[64,24,128]{2,1,0:T(8,128)}), f32[64,24,128]{2,1,0:T(8,128)S(1)}, u32[]{:S(2)}, u32[]{:S(2)}) async-start(f32[64,24,128]{2,1,0:T(8,128)} %copy.54), calls=%async_computation | async-start | bytes 1572864 | tf_op jit(solution)/shard_map/all_to_all | solution.py:18
  18.5 0.7 copy-start.4
  43.1 9.9 %collective-permute-start.1 = (f32[192,128]{1,0:T(8,128)S(1)}, f32[192,128]{1,0:T(8,128)S(1)}, u32[]{:S(2)}, u32[]{:S(2)}) collective-permute-start(f32[192,128]{1,0:T(8,128)S(1)} %reshape.196), channel_id=1, source_target_pairs={{1,0},{2,1},{3,2},{4,3},{5,4},{6,5},{7,6},{9,8},{10,9},{11,10},{12... | collective-permute-start | bytes 294920 | tf_op jit(solution)/shard_map/ppermute | solution.py:36
  48.6 5.8 %collective-permute-start = (f32[192,128]{1,0:T(8,128)S(1)}, f32[192,128]{1,0:T(8,128)S(1)}, u32[]{:S(2)}, u32[]{:S(2)}) collective-permute-start(f32[192,128]{1,0:T(8,128)S(1)} %reshape.194), channel_id=1, source_target_pairs={{0,1},{1,2},{2,3},{3,4},{4,5},{5,6},{6,7},{8,9},{9,10},{10,11},{11... | collective-permute-start | bytes 294920 | tf_op jit(solution)/shard_map/ppermute | solution.py:36
  58.1 7.9 %copy-start.2 = (s32[8,160]{1,0:T(8,128)S(1)}, s32[8,160]{1,0:T(8,128)}, u32[]{:S(2)}) copy-start(s32[8,160]{1,0:T(8,128)} %param.10) | copy-start | bytes 15364
  58.1 18.3 %all-to-all-start.1 = ((f32[64,8,128]{2,1,0:T(8,128)}), f32[64,8,128]{2,1,0:T(8,128)S(1)}, u32[]{:S(2)}, u32[]{:S(2)}) async-start(f32[64,8,128]{2,1,0:T(8,128)} %bitcast.14), calls=%async_computation.1 | async-start | bytes 524288 | tf_op jit(solution)/shard_map/all_to_all | solution.py:44
  64.7 0.7 copy-start.3
  77.2 16.0 %all-to-all-start.2 = ((f32[64,8,128]{2,1,0:T(8,128)}), f32[64,8,128]{2,1,0:T(8,128)S(1)}, u32[]{:S(2)}, u32[]{:S(2)}) async-start(f32[64,8,128]{2,1,0:T(8,128)} %broadcast_in_dim.15), calls=%async_computation.2 | async-start | bytes 524288 | tf_op jit(solution)/shard_map/all_to_all | solution.py:45
  97.2 10.6 %collective-permute-start.3 = (f32[128,128]{1,0:T(8,128)S(1)}, f32[128,128]{1,0:T(8,128)S(1)}, u32[]{:S(2)}, u32[]{:S(2)}) collective-permute-start(f32[128,128]{1,0:T(8,128)S(1)} %reshape.203), channel_id=1, source_target_pairs={{1,0},{2,1},{3,2},{4,3},{5,4},{6,5},{7,6},{9,8},{10,9},{11,10},{12... | collective-permute-start | bytes 196616 | tf_op jit(solution)/shard_map/ppermute | solution.py:36
  102.4 6.7 %collective-permute-start.2 = (f32[128,128]{1,0:T(8,128)S(1)}, f32[128,128]{1,0:T(8,128)S(1)}, u32[]{:S(2)}, u32[]{:S(2)}) collective-permute-start(f32[128,128]{1,0:T(8,128)S(1)} %reshape.201), channel_id=1, source_target_pairs={{0,1},{1,2},{2,3},{3,4},{4,5},{5,6},{6,7},{8,9},{9,10},{10,11},{11... | collective-permute-start | bytes 196616 | tf_op jit(solution)/shard_map/ppermute | solution.py:36
  127.3 16.3 %all-to-all-start.4 = ((f32[64,8,128]{2,1,0:T(8,128)}), f32[64,8,128]{2,1,0:T(8,128)S(1)}, u32[]{:S(2)}, u32[]{:S(2)}) async-start(f32[64,8,128]{2,1,0:T(8,128)} %broadcast_in_dim.33), calls=%async_computation.4 | async-start | bytes 524288 | tf_op jit(solution)/shard_map/all_to_all | solution.py:45
  147.8 11.3 %collective-permute-start.5 = (f32[64,128]{1,0:T(8,128)S(1)}, f32[64,128]{1,0:T(8,128)S(1)}, u32[]{:S(2)}, u32[]{:S(2)}) collective-permute-start(f32[64,128]{1,0:T(8,128)S(1)} %reshape.211), channel_id=1, source_target_pairs={{1,0},{2,1},{3,2},{4,3},{5,4},{6,5},{7,6},{9,8},{10,9},{11,10},{12... | collective-permute-start | bytes 98312 | tf_op jit(solution)/shard_map/ppermute | solution.py:36
  150.1 10.0 %collective-permute-start.4 = (f32[64,128]{1,0:T(8,128)S(1)}, f32[64,128]{1,0:T(8,128)S(1)}, u32[]{:S(2)}, u32[]{:S(2)}) collective-permute-start(f32[64,128]{1,0:T(8,128)S(1)} %reshape.209), channel_id=1, source_target_pairs={{0,1},{1,2},{2,3},{3,4},{4,5},{5,6},{6,7},{8,9},{9,10},{10,11},{11... | collective-permute-start | bytes 98312 | tf_op jit(solution)/shard_map/ppermute | solution.py:36

commit v2 on v1

v2 whole, which is shorter than its diff:
```python
import math

import jax
import jax.numpy as jnp
from jax import lax
from jax.experimental import pallas as pl
from jax.experimental.pallas import tpu as pltpu
from jax.sharding import PartitionSpec as P


OV = 16
CL = 4
WL = 2
HD = 128
G8 = CL * WL
ARRAYS = 3
HI = lax.Precision.HIGHEST
F32 = jnp.float32


def lanes(shape):
    return lax.broadcasted_iota(jnp.int32, shape, 1)


def shift(x, by):
    by %= x.shape[1]
    return pltpu.roll(x, by, 1) if by else x


def pack_center(pieces, offset):
    group = lanes(pieces[0].shape) // OV
    out = shift(pieces[0], -offset)
    for g in range(1, G8):
        out = jnp.where(group == g, shift(pieces[g], OV * g - offset), out)
    return out


def pack_edges(edges, offset):
    group = lanes(edges[0].shape) // (WL * OV)
    out = shift(edges[0], -offset)
    for c in range(1, CL):
        out = jnp.where(group == c, shift(edges[c], WL * OV * c - offset), out)
    return out


def open_edges(before, after, c):
    lane = lanes(before.shape)
    step = WL * OV
    rest = jnp.where(lane < 2 * step, shift(after, step - step * c), 0.0)
    return jnp.where(lane < step, shift(before, -step * c), rest)


def open_center(before, after, g):
    lane = lanes(before.shape)
    rest = jnp.where(lane >= HD - OV, shift(after, HD - OV - OV * g), 0.0)
    return jnp.where(lane < OV, shift(before, -OV * g), rest)


def gram_of(x):
    return lax.dot_general(x, x, (((1,), (1,)), ((), ())), precision=HI, preferred_element_type=F32)


def pack_body(est, dirty, weights, out):
    n = out.shape[0] // (ARRAYS * G8)
    for c in range(CL):
        for w in range(WL):
            rows = pl.ds(c * WL * n + w, n, stride=WL)
            e, d, k = est[rows, :], dirty[rows, :], weights[rows, :]
            for a, value in enumerate((e - k * (e - d), d, k)):
                out[pl.ds(a * G8 + c * WL + w, n, stride=ARRAYS * G8), :] = value


def piece(got, a, g):
    n = got.shape[0] // (ARRAYS * G8)
    return got[pl.ds(a * G8 + g, n, stride=ARRAYS * G8), :]


def edge_body(got, low, high):
    n = low.shape[0] // ARRAYS
    for a in range(ARRAYS):
        pieces = [piece(got, a, g) for g in range(G8)]
        low[pl.ds(a * n, n), :] = pack_center(pieces, 0)
        high[pl.ds(a * n, n), :] = pack_center(pieces, HD - OV)


def gram_body(got, before, after, table, x, gram):
    n = before.shape[0] // ARRAYS
    keep = table[0:1, WL * HD :]
    for c in range(CL):
        rows = pl.ds(c * n, n)
        for w in range(WL):
            x[rows, pl.ds(w * HD, HD)] = piece(got, 0, c * WL + w)
        x[rows, pl.ds(WL * HD, HD)] = open_edges(before[pl.ds(0, n), :], after[pl.ds(0, n), :], c) * keep
    gram[...] = gram_of(x[...])


def shrink_of(gram, x, factor):
    count = gram.shape[0]
    row = lax.broadcasted_iota(jnp.int32, gram.shape, 0)
    identity = (row == lanes(gram.shape)).astype(F32)
    trace = jnp.sum(jnp.sum(gram * identity, axis=1, keepdims=True), axis=0, keepdims=True)
    mean_eigen = trace / count + 1e-06
    target = (gram + (0.01 * mean_eigen) * identity) / (16.16 * mean_eigen)
    first = 1.5 * identity - 0.5 * target
    target = jnp.dot(target, first, precision=HI)
    second = 1.5 * identity - 0.5 * jnp.dot(first, target, precision=HI)
    inverse_root = jnp.dot(second, first, precision=HI)
    return jnp.dot(identity - factor * inverse_root, x, precision=HI)


def apply_body(step, last, gram, x, table, out, low, high):
    n = x.shape[0] // CL
    factor = table[3 + step : 4 + step, : gram.shape[0]]
    out[...] = shrink_of(gram[...], x[...], factor) * table[1:2, :]
    edges = [out[pl.ds(c * n, n), pl.ds(WL * HD, HD)] for c in range(CL)]
    inner = slice(0, n) if last else slice(n, 2 * n)
    low[inner, :] = pack_edges(edges, 0)
    high[inner, :] = pack_edges(edges, WL * OV)
    if not last:
        pieces = [out[pl.ds(c * n, n), pl.ds(w * HD, HD)] for c in range(CL) for w in range(WL)]
        low[0:n, :] = pack_center(pieces, 0)
        high[0:n, :] = pack_center(pieces, HD - OV)


def next_body(got, before, after, s, s_before, s_after, table, x, gram):
    n = before.shape[0] // ARRAYS
    keep = table[0:1, WL * HD :]
    scale = table[2:3, :]
    for c in range(CL):
        rows = pl.ds(c * n, n)

        def moved(total, cols, d, k):
            current = total * scale[:, cols]
            return current - k * (current - d)

        for w in range(WL):
            g = c * WL + w
            cols = slice(w * HD, w * HD + HD)
            total = s[rows, cols] + open_center(s_before[n : 2 * n, :], s_after[n : 2 * n, :], g)
            x[rows, cols] = moved(total, cols, piece(got, 1, g), piece(got, 2, g))
        cols = slice(WL * HD, WL * HD + HD)
        total = s[rows, cols] + open_edges(s_before[0:n, :], s_after[0:n, :], c)
        d = open_edges(before[n : 2 * n, :], after[n : 2 * n, :], c)
        k = open_edges(before[2 * n :, :], after[2 * n :, :], c)
        x[rows, cols] = moved(total, cols, d, k) * keep
    gram[...] = gram_of(x[...])


def close_body(s, s_before, s_after, table, out):
    n = s_before.shape[0]
    for c in range(CL):
        for w in range(WL):
            g = c * WL + w
            total = s[pl.ds(c * n, n), pl.ds(w * HD, HD)] + open_center(s_before[...], s_after[...], g)
            out[pl.ds(g, n, stride=G8), :] = total * table[2:3, w * HD : w * HD + HD]


def unpack_body(got, out):
    n = got.shape[0] // G8
    for c in range(CL):
        for w in range(WL):
            out[pl.ds(c * WL * n + w, n, stride=WL), :] = got[pl.ds(c * WL + w, n, stride=G8), :]


def run(body, name, shapes, *args, enter=True, leave=True):
    spec = pl.BlockSpec(memory_space=pltpu.VMEM)
    outs = [pltpu.VMEM(s, F32) if leave else jax.ShapeDtypeStruct(s, F32) for s in shapes]
    single = len(outs) == 1
    if enter:
        args = [pltpu.with_memory_space_constraint(a, pltpu.VMEM) for a in args]
    return pl.pallas_call(
        body,
        out_shape=outs[0] if single else outs,
        in_specs=[spec] * len(args),
        out_specs=spec if single else [spec] * len(outs),
        name=name,
    )(*args)


def exchange(x, n):
    return lax.all_to_all(x.reshape(n, -1, HD), "chan", 0, 0).reshape(x.shape)


def swap(low, high):
    size = lax.axis_size("facet")
    up = [(i, i + 1) for i in range(size - 1)]
    down = [(i + 1, i) for i in range(size - 1)]
    return lax.ppermute(high, "facet", up), lax.ppermute(low, "facet", down)


def total_gram(partial, n):
    c = partial.shape[0]
    tiles = partial.reshape(c // 8, 8, c // 128, 128).transpose(0, 2, 1, 3).reshape(n, -1, 128)
    mine = jnp.sum(lax.all_to_all(tiles, "chan", 0, 0), axis=0)
    every = lax.all_to_all(jnp.broadcast_to(mine[None], tiles.shape), "chan", 0, 0)
    return every.reshape(c // 8, c // 128, 8, 128).transpose(0, 2, 1, 3).reshape(c, c)


def tables(margin, blend_table, tau_steps, channels):
    facet_id = lax.axis_index("facet")
    facet_total = lax.axis_size("facet")
    row_index = jnp.arange(HD + 2 * OV, dtype=jnp.int32)[None, :]
    keep_all = (
        (row_index >= OV - margin[:, None]) & (row_index < HD + OV + margin[:, None])
    ).astype(F32)
    weight_all = blend_table.astype(F32) * keep_all
    row_weight = weight_all[facet_id]
    before = weight_all[jnp.maximum(facet_id - 1, 0)][HD:] * (facet_id > 0)
    after = weight_all[jnp.minimum(facet_id + 1, facet_total - 1)][: 2 * OV] * (
        facet_id < facet_total - 1
    )
    total = row_weight + jnp.concatenate([before, jnp.zeros((HD - 2 * OV,), F32), after])
    scale = 1.0 / jnp.where(total == 0.0, 1.0, total)
    rows = jnp.stack([keep_all[facet_id], row_weight, scale])
    center, low, high = rows[:, OV : OV + HD], rows[:, :OV], rows[:, OV + HD :]
    pad = jnp.zeros((3, HD - 4 * OV), F32)
    rows = jnp.concatenate([center, center, low, low, high, high, pad], axis=1)
    factors = 0.1 * tau_steps.astype(F32) / math.sqrt(1.01)
    factors = jnp.broadcast_to(factors[:, None], (tau_steps.shape[0], rows.shape[1]))
    return jnp.concatenate([rows, factors, jnp.zeros((3, rows.shape[1]), F32)])


def per_device(estimate, dirty, weights, margin, blend_table, tau_steps):
    n = lax.axis_size("chan")
    c, width = n * CL, (WL + 1) * HD
    assert estimate.shape == (CL, n * WL, HD)
    table = tables(margin, blend_table, tau_steps, c)
    flat = (CL * WL * n, HD)
    sent = run(
        pack_body, "pack", [(ARRAYS * G8 * n, HD)], estimate.reshape(flat), dirty.reshape(flat), weights.reshape(flat), enter=False
    )
    got = exchange(sent, n)
    low, high = run(edge_body, "edges", [(ARRAYS * n, HD)] * 2, got)
    before, after = swap(low, high)
    x, gram = run(gram_body, "gram", [(c, width), (c, c)], got, before, after, table)
    gram = total_gram(gram, n)
    s, low, high = run(
        lambda *refs: apply_body(0, False, *refs), "shrink", [(c, width), (2 * n, HD), (2 * n, HD)], gram, x, table
    )
    s_before, s_after = swap(low, high)
    x, gram = run(
        next_body, "step", [(c, width), (c, c)], got, before, after, s, s_before, s_after, table
    )
    gram = total_gram(gram, n)
    s, low, high = run(
        lambda *refs: apply_body(1, True, *refs), "last", [(c, width), (n, HD), (n, HD)], gram, x, table
    )
    s_before, s_after = swap(low, high)
    back = exchange(run(close_body, "close", [(G8 * n, HD)], s, s_before, s_after, table), n)
    return run(unpack_body, "unpack", [flat], back, leave=False).reshape(estimate.shape)


def solution(mesh):
    placed = (
        P("chan", None, "facet"),
        P("chan", None, "facet"),
        P("chan", None, "facet"),
        P(),
        P(),
        P(),
    )
    return jax.shard_map(
        per_device, mesh=mesh, in_specs=placed, out_specs=P("chan", None, "facet"), check_vma=False
    )
```

time: 180 us -> 165 us (0.917); the launches traced: 177 us -> 164 us
  blocking collectives: 30.5 us -> 82.5 us
  starting transfers between devices: 60.3 us -> 35.2 us
  waiting for transfers between devices: 54.5 us -> 35.4 us
  local copies, waits for them, and re-layouts: 18.1 us -> 1.13 us
  Pallas kernels: 0 us -> 9.49 us
  matrix products: 6.34 us -> 0 us
  other arithmetic: 4.04 us -> 0.48 us
  between operations: 3.11 us -> 0.19 us
    all_to_all x1 -> x3, blocking collectives: 15 us -> 50.8 us  [the longest x2 33.5 us: total_gram(): lax.all_to_all(jnp.broadcast_to(mine[None], tiles.shape), 'chan', 0, 0)]
    all_to_all x4 -> x1, waiting for transfers between devices: 53 us -> 20.7 us  [exchange(): return lax.all_to_all(x.reshape(n, -1, HD), 'chan', 0, 0).reshape(x.shape)]
    all_to_all x1 -> x2, blocking collectives: 15.5 us -> 31.7 us  [total_gram(): mine = jnp.sum(lax.all_to_all(tiles, 'chan', 0, 0), axis=0)]
    all_to_all x4 -> x1, starting transfers between devices: 31.4 us -> 15.5 us  [exchange(): return lax.all_to_all(x.reshape(n, -1, HD), 'chan', 0, 0).reshape(x.shape)]
    ppermute x6, waiting for transfers between devices: 1.49 us -> 14.6 us  [swap(): return (lax.ppermute(high, 'facet', up), lax.ppermute(low, 'facet', down))]
    pallas_call x0 -> x8, Pallas kernels: none -> 9.49 us  [run(): pl.pallas_call(body, out_shape=outs[0] if single else outs, in_specs=[spe...]
    ppermute x6, starting transfers between devices: 28.9 us -> 19.8 us  [swap(): return (lax.ppermute(high, 'facet', up), lax.ppermute(low, 'facet', down))]
    reshape x20 -> x0, local copies, waits for them, and re-layouts: 8.92 us -> none  [the longest x18 7.28 us: move(): return lax.ppermute(x.reshape(-1, 128), 'facet', pairs).reshape(shape)]
  transfers between devices with their start and end apart: 10 -> 7, of which waited for: 6 -> 4; matrix products, arithmetic and copies ran while one was open for 3% -> 0% of each run, Pallas kernels for 0% -> 0%
where the time goes in v2:
time: 165 us; the launch traced here: 164 us
  blocking collectives  82.5 us (50%)
  waiting for transfers between devices  35.4 us (21%)
  starting transfers between devices  35.2 us (21%)
  Pallas kernels  9.49 us (6%)
    all_to_all x2, blocking collectives, total_gram(): lax.all_to_all(jnp.broadcast_to(mine[None], tiles.shape), 'chan', 0, 0)  33.5 us
    all_to_all x2, blocking collectives, total_gram(): mine = jnp.sum(lax.all_to_all(tiles, 'chan', 0, 0), axis=0)  31.7 us
    all_to_all x1, waiting for transfers between devices, exchange(): return lax.all_to_all(x.reshape(n, -1, HD), 'chan', 0, 0).reshape(x.shape)  20.7 us
    ppermute x6, starting transfers between devices, swap(): return (lax.ppermute(high, 'facet', up), lax.ppermute(low, 'facet', down))  19.8 us
    all_to_all x1, blocking collectives, exchange(): return lax.all_to_all(x.reshape(n, -1, HD), 'chan', 0, 0).reshape(x.shape)  17.3 us
    all_to_all x1, starting transfers between devices, exchange(): return lax.all_to_all(x.reshape(n, -1, HD), 'chan', 0, 0).reshape(x.shape)  15.5 us
    ppermute x6, waiting for transfers between devices, swap(): return (lax.ppermute(high, 'facet', up), lax.ppermute(low, 'facet', down))  14.6 us
    pallas_call x8, Pallas kernels, run(): pl.pallas_call(body, out_shape=outs[0] if single else outs, in_specs=[spe...  9.49 us
  transfers between devices with their start and end apart: 7, of which 4 were waited for; matrix products, arithmetic and copies ran while one was open for 0% of the time, Pallas kernels for 0%

profile of v2, /device:TPU:1, one launch (start us, length us, event | category | flops | bytes accessed | tf_op | source)
XLA Modules:
  0.0 164.4 jit_solution(16497356080695043053)
XLA Ops:
  0.0 2.2 %pack.1 = f32[1536,128]{1,0:T(8,128)} custom-call(f32[512,128]{1,0:T(8,128)} %bitcast.38, f32[512,128]{1,0:T(8,128)} %bitcast.39, f32[512,128]{1,0:T(8,128)} %bitcast.40), custom_call_target="tpu_custom_call" | custom-call | tf_op jit(solution)/shard_map/pack/pallas_call | solution.py:171
  2.2 15.5 %all-to-all-start = ((f32[64,24,128]{2,1,0:T(8,128)}), f32[64,24,128]{2,1,0:T(8,128)S(1)}, u32[]{:S(2)}, u32[]{:S(2)}) async-start(f32[64,24,128]{2,1,0:T(8,128)} %bitcast.3), calls=%async_computation | async-start | bytes 1572864 | tf_op jit(solution)/shard_map/all_to_all | solution.py:181
  17.8 0.1 pad.1.clone
  17.8 0.1 pad.2.clone
  17.9 0.1 pad.7.clone
  18.0 0.4 copy-done.2
  18.4 0.1 fusion
  18.5 0.2 copy-done
  18.8 0.1 dynamic-slice_multiply_fusion
  19.0 0.1 concatenate.11
  19.1 20.7 %all-to-all-done = f32[64,24,128]{2,1,0:T(8,128)S(1)} async-done(((f32[64,24,128]{2,1,0:T(8,128)}), f32[64,24,128]{2,1,0:T(8,128)S(1)}, u32[]{:S(2)}, u32[]{:S(2)}) %all-to-all-start) | async-done | bytes 786464 | tf_op jit(solution)/shard_map/all_to_all | solution.py:181
  39.8 0.4 edges.1
  40.3 6.2 %collective-permute-start = (f32[192,128]{1,0:T(8,128)S(1)}, f32[192,128]{1,0:T(8,128)S(1)}, u32[]{:S(2)}, u32[]{:S(2)}) collective-permute-start(f32[192,128]{1,0:T(8,128)S(1)} %get-tuple-element.17), channel_id=1, source_target_pairs={{0,1},{1,2},{2,3},{3,4},{4,5},{5,6},{6,7},{8,9},{9,10},{10,11},{11... | collective-permute-start | bytes 294920 | tf_op jit(solution)/shard_map/ppermute | solution.py:188
  46.4 1.9 %collective-permute-start.1 = (f32[192,128]{1,0:T(8,128)S(1)}, f32[192,128]{1,0:T(8,128)S(1)}, u32[]{:S(2)}, u32[]{:S(2)}) collective-permute-start(f32[192,128]{1,0:T(8,128)S(1)} %get-tuple-element.18), channel_id=1, source_target_pairs={{1,0},{2,1},{3,2},{4,3},{5,4},{6,5},{7,6},{9,8},{10,9},{11,10},{12... | collective-permute-start | bytes 294920 | tf_op jit(solution)/shard_map/ppermute | solution.py:188
  48.4 5.9 %collective-permute-done.1.after = f32[192,128]{1,0:T(8,128)S(1)} collective-permute-done((f32[192,128]{1,0:T(8,128)S(1)}, f32[192,128]{1,0:T(8,128)S(1)}, u32[]{:S(2)}, u32[]{:S(2)}) %collective-permute-start.1) | collective-permute-done | bytes 98336 | tf_op jit(solution)/shard_map/ppermute | solution.py:188
  54.3 0.7 gram.1
  55.0 14.5 %all_to_all.30 = f32[64,8,128]{2,1,0:T(8,128)S(1)} all-to-all(f32[64,8,128]{2,1,0:T(8,128)S(1)} %bitcast.37), channel_id=1, replica_groups=mesh['chan'=64,'facet'=8] {'chan'}, dimensions={0} | all-to-all | bytes 524288 | tf_op jit(solution)/shard_map/all_to_all | solution.py:194
  69.6 16.9 %all_to_all.31 = f32[64,8,128]{2,1,0:T(8,128)S(1)} all-to-all(f32[64,8,128]{2,1,0:T(8,128)S(1)} %broadcast_in_dim.18), channel_id=1, replica_groups=mesh['chan'=64,'facet'=8] {'chan'}, dimensions={0} | all-to-all | bytes 524288 | tf_op jit(solution)/shard_map/all_to_all | solution.py:195
  86.4 2.2 %shrink.1 = (f32[256,384]{1,0:T(8,128)S(1)}, f32[128,128]{1,0:T(8,128)S(1)}, f32[128,128]{1,0:T(8,128)S(1)}) custom-call(f32[256,256]{1,0:T(8,128)S(1)} %bitcast.33, f32[256,384]{1,0:T(8,128)S(1)} %get-tuple-element.20.refs_1_, f32[8,384]{1,0:T(8,128)S(1)} %maximum_maximum_fusion.table.refs_2_), custom_call_target="tpu_custom_call" | custom-call | tf_op jit(solution)/shard_map/shrink/pallas_call | solution.py:171
  88.7 3.7 %collective-permute-start.2 = (f32[128,128]{1,0:T(8,128)S(1)}, f32[128,128]{1,0:T(8,128)S(1)}, u32[]{:S(2)}, u32[]{:S(2)}) collective-permute-start(f32[128,128]{1,0:T(8,128)S(1)} %get-tuple-element.22), channel_id=1, source_target_pairs={{0,1},{1,2},{2,3},{3,4},{4,5},{5,6},{6,7},{8,9},{9,10},{10,11},{11... | collective-permute-start | bytes 196616 | tf_op jit(solution)/shard_map/ppermute | solution.py:188
  92.3 1.9 %collective-permute-start.3 = (f32[128,128]{1,0:T(8,128)S(1)}, f32[128,128]{1,0:T(8,128)S(1)}, u32[]{:S(2)}, u32[]{:S(2)}) collective-permute-start(f32[128,128]{1,0:T(8,128)S(1)} %get-tuple-element.23), channel_id=1, source_target_pairs={{1,0},{2,1},{3,2},{4,3},{5,4},{6,5},{7,6},{9,8},{10,9},{11,10},{12... | collective-permute-start | bytes 196616 | tf_op jit(solution)/shard_map/ppermute | solution.py:188
  94.3 4.5 %collective-permute-done.3.s_after = f32[128,128]{1,0:T(8,128)S(1)} collective-permute-done((f32[128,128]{1,0:T(8,128)S(1)}, f32[128,128]{1,0:T(8,128)S(1)}, u32[]{:S(2)}, u32[]{:S(2)}) %collective-permute-start.3) | collective-permute-done | bytes 65568 | tf_op jit(solution)/shard_map/ppermute | solution.py:188
  98.8 0.9 step.1
  99.7 17.2 %all_to_all.32 = f32[64,8,128]{2,1,0:T(8,128)S(1)} all-to-all(f32[64,8,128]{2,1,0:T(8,128)S(1)} %bitcast.36), channel_id=1, replica_groups=mesh['chan'=64,'facet'=8] {'chan'}, dimensions={0} | all-to-all | bytes 524288 | tf_op jit(solution)/shard_map/all_to_all | solution.py:194
  117.1 16.6 %all_to_all.33 = f32[64,8,128]{2,1,0:T(8,128)S(1)} all-to-all(f32[64,8,128]{2,1,0:T(8,128)S(1)} %broadcast_in_dim.19), channel_id=1, replica_groups=mesh['chan'=64,'facet'=8] {'chan'}, dimensions={0} | all-to-all | bytes 524288 | tf_op jit(solution)/shard_map/all_to_all | solution.py:195
  133.7 2.1 %last.1 = (f32[256,384]{1,0:T(8,128)S(1)}, f32[64,128]{1,0:T(8,128)S(1)}, f32[64,128]{1,0:T(8,128)S(1)}) custom-call(f32[256,256]{1,0:T(8,128)S(1)} %bitcast.34, f32[256,384]{1,0:T(8,128)S(1)} %get-tuple-element.25.refs_1_, f32[8,384]{1,0:T(8,128)S(1)} %maximum_maximum_fusion.table.refs_2_), custom_call_target="tpu_custom_call" | custom-call | tf_op jit(solution)/shard_map/last/pallas_call | solution.py:171
  135.8 4.2 %collective-permute-start.4 = (f32[64,128]{1,0:T(8,128)S(1)}, f32[64,128]{1,0:T(8,128)S(1)}, u32[]{:S(2)}, u32[]{:S(2)}) collective-permute-start(f32[64,128]{1,0:T(8,128)S(1)} %get-tuple-element.27), channel_id=1, source_target_pairs={{0,1},{1,2},{2,3},{3,4},{4,5},{5,6},{6,7},{8,9},{9,10},{10,11},{11... | collective-permute-start | bytes 98312 | tf_op jit(solution)/shard_map/ppermute | solution.py:188
  140.1 1.9 %collective-permute-start.5 = (f32[64,128]{1,0:T(8,128)S(1)}, f32[64,128]{1,0:T(8,128)S(1)}, u32[]{:S(2)}, u32[]{:S(2)}) collective-permute-start(f32[64,128]{1,0:T(8,128)S(1)} %get-tuple-element.28), channel_id=1, source_target_pairs={{1,0},{2,1},{3,2},{4,3},{5,4},{6,5},{7,6},{9,8},{10,9},{11,10},{12... | collective-permute-start | bytes 98312 | tf_op jit(solution)/shard_map/ppermute | solution.py:188
  142.0 4.2 %collective-permute-done.5.s_after = f32[64,128]{1,0:T(8,128)S(1)} collective-permute-done((f32[64,128]{1,0:T(8,128)S(1)}, f32[64,128]{1,0:T(8,128)S(1)}, u32[]{:S(2)}, u32[]{:S(2)}) %collective-permute-start.5) | collective-permute-done | bytes 32800 | tf_op jit(solution)/shard_map/ppermute | solution.py:188
  146.2 0.2 close.1
  146.4 17.3 %all_to_all.34 = f32[64,8,128]{2,1,0:T(8,128)S(1)} all-to-all(f32[64,8,128]{2,1,0:T(8,128)S(1)} %bitcast.35), channel_id=1, replica_groups=mesh['chan'=64,'facet'=8] {'chan'}, dimensions={0} | all-to-all | bytes 524288 | tf_op jit(solution)/shard_map/all_to_all | solution.py:181
  163.7 0.8 unpack.1
  (23 shorter events, 0.5 us)
Async XLA Ops:
  2.2 15.5 %copy-start.1 = (s32[2]{0:T(128)S(1)}, s32[2]{0:T(128)}, u32[]{:S(2)}) copy-start(s32[2]{0:T(128)} %param.11) | copy-start | bytes 28
  2.2 37.6 %all-to-all-start = ((f32[64,24,128]{2,1,0:T(8,128)}), f32[64,24,128]{2,1,0:T(8,128)S(1)}, u32[]{:S(2)}, u32[]{:S(2)}) async-start(f32[64,24,128]{2,1,0:T(8,128)} %bitcast.3), calls=%async_computation | async-start | bytes 1572864 | tf_op jit(solution)/shard_map/all_to_all | solution.py:181
  17.7 0.7 copy-start.2
  18.0 0.7 copy-start
  40.3 8.2 %collective-permute-start = (f32[192,128]{1,0:T(8,128)S(1)}, f32[192,128]{1,0:T(8,128)S(1)}, u32[]{:S(2)}, u32[]{:S(2)}) collective-permute-start(f32[192,128]{1,0:T(8,128)S(1)} %get-tuple-element.17), channel_id=1, source_target_pairs={{0,1},{1,2},{2,3},{3,4},{4,5},{5,6},{6,7},{8,9},{9,10},{10,11},{11... | collective-permute-start | bytes 294920 | tf_op jit(solution)/shard_map/ppermute | solution.py:188
  46.4 7.9 %collective-permute-start.1 = (f32[192,128]{1,0:T(8,128)S(1)}, f32[192,128]{1,0:T(8,128)S(1)}, u32[]{:S(2)}, u32[]{:S(2)}) collective-permute-start(f32[192,128]{1,0:T(8,128)S(1)} %get-tuple-element.18), channel_id=1, source_target_pairs={{1,0},{2,1},{3,2},{4,3},{5,4},{6,5},{7,6},{9,8},{10,9},{11,10},{12... | collective-permute-start | bytes 294920 | tf_op jit(solution)/shard_map/ppermute | solution.py:188
  88.7 5.6 %collective-permute-start.2 = (f32[128,128]{1,0:T(8,128)S(1)}, f32[128,128]{1,0:T(8,128)S(1)}, u32[]{:S(2)}, u32[]{:S(2)}) collective-permute-start(f32[128,128]{1,0:T(8,128)S(1)} %get-tuple-element.22), channel_id=1, source_target_pairs={{0,1},{1,2},{2,3},{3,4},{4,5},{5,6},{6,7},{8,9},{9,10},{10,11},{11... | collective-permute-start | bytes 196616 | tf_op jit(solution)/shard_map/ppermute | solution.py:188
  92.3 6.5 %collective-permute-start.3 = (f32[128,128]{1,0:T(8,128)S(1)}, f32[128,128]{1,0:T(8,128)S(1)}, u32[]{:S(2)}, u32[]{:S(2)}) collective-permute-start(f32[128,128]{1,0:T(8,128)S(1)} %get-tuple-element.23), channel_id=1, source_target_pairs={{1,0},{2,1},{3,2},{4,3},{5,4},{6,5},{7,6},{9,8},{10,9},{11,10},{12... | collective-permute-start | bytes 196616 | tf_op jit(solution)/shard_map/ppermute | solution.py:188
  135.8 6.2 %collective-permute-start.4 = (f32[64,128]{1,0:T(8,128)S(1)}, f32[64,128]{1,0:T(8,128)S(1)}, u32[]{:S(2)}, u32[]{:S(2)}) collective-permute-start(f32[64,128]{1,0:T(8,128)S(1)} %get-tuple-element.27), channel_id=1, source_target_pairs={{0,1},{1,2},{2,3},{3,4},{4,5},{5,6},{6,7},{8,9},{9,10},{10,11},{11... | collective-permute-start | bytes 98312 | tf_op jit(solution)/shard_map/ppermute | solution.py:188
  140.1 6.1 %collective-permute-start.5 = (f32[64,128]{1,0:T(8,128)S(1)}, f32[64,128]{1,0:T(8,128)S(1)}, u32[]{:S(2)}, u32[]{:S(2)}) collective-permute-start(f32[64,128]{1,0:T(8,128)S(1)} %get-tuple-element.28), channel_id=1, source_target_pairs={{1,0},{2,1},{3,2},{4,3},{5,4},{6,5},{7,6},{9,8},{10,9},{11,10},{12... | collective-permute-start | bytes 98312 | tf_op jit(solution)/shard_map/ppermute | solution.py:188

commit v3 on v2

v3 whole, which is shorter than its diff:
```python
import math

import jax
import jax.numpy as jnp
from jax import lax
from jax.experimental import pallas as pl
from jax.experimental.pallas import tpu as pltpu
from jax.sharding import PartitionSpec as P


OV = 16
CL = 4
WL = 2
HD = 128
G8 = CL * WL
ARRAYS = 3
F32 = jnp.float32


def lanes(shape):
    return lax.broadcasted_iota(jnp.int32, shape, 1)


def shift(x, by):
    by %= x.shape[1]
    return pltpu.roll(x, by, 1) if by else x


def pack_center(pieces, offset):
    group = lanes(pieces[0].shape) // OV
    out = shift(pieces[0], -offset)
    for g in range(1, G8):
        out = jnp.where(group == g, shift(pieces[g], OV * g - offset), out)
    return out


def pack_edges(edges, offset):
    group = lanes(edges[0].shape) // (WL * OV)
    out = shift(edges[0], -offset)
    for c in range(1, CL):
        out = jnp.where(group == c, shift(edges[c], WL * OV * c - offset), out)
    return out


def open_edges(before, after, c):
    lane = lanes(before.shape)
    step = WL * OV
    rest = jnp.where(lane < 2 * step, shift(after, step - step * c), 0.0)
    return jnp.where(lane < step, shift(before, -step * c), rest)


def open_center(before, after, g):
    lane = lanes(before.shape)
    rest = jnp.where(lane >= HD - OV, shift(after, HD - OV - OV * g), 0.0)
    return jnp.where(lane < OV, shift(before, -OV * g), rest)


def split(x):
    top = x.astype(jnp.bfloat16)
    return top, (x - top.astype(F32)).astype(jnp.bfloat16)


def product(a, b, contract=((1,), (0,))):
    dims = (contract, ((), ()))
    parts = ((a[0], b[1]), (a[1], b[0]), (a[0], b[0]))
    p, q, r = (lax.dot_general(u, v, dims, preferred_element_type=F32) for u, v in parts)
    return p + q + r


def put_gram(x, tri):
    half = x.shape[0] // 2
    parts = split(x[...])
    low, high = ([p[i * half : i * half + half, :] for p in parts] for i in (0, 1))
    rows = ((1,), (1,))
    first, second = product(low, low, rows), product(high, high, rows)
    row = lax.broadcasted_iota(jnp.int32, first.shape, 0)
    col = lanes(first.shape)
    tri[0:half, :] = product(low, high, rows)
    tri[half : 2 * half, :] = jnp.where(row >= col, first, second)
    diagonal = jnp.sum(jnp.where(row == col, second, 0.0), axis=0, keepdims=True)
    rest = (tri.shape[0] - 2 * half, half)
    tri[2 * half :, :] = jnp.where(lax.broadcasted_iota(jnp.int32, rest, 0) == 0, diagonal, 0.0)


def get_gram(tri, gram):
    half = gram.shape[0] // 2
    above, both = tri[0:half, :], tri[half : 2 * half, :]
    row = lax.broadcasted_iota(jnp.int32, both.shape, 0)
    col = lanes(both.shape)
    turned = both.T
    gram[0:half, 0:half] = jnp.where(row >= col, both, turned)
    gram[0:half, half:] = above
    gram[half:, 0:half] = above.T
    diagonal = jnp.where(row == col, tri[2 * half : 2 * half + 1, :], turned)
    gram[half:, half:] = jnp.where(row < col, both, diagonal)
    return gram[...]


def pack_body(est, dirty, weights, out):
    n = out.shape[0] // (ARRAYS * G8)
    for c in range(CL):
        for w in range(WL):
            rows = pl.ds(c * WL * n + w, n, stride=WL)
            e, d, k = est[rows, :], dirty[rows, :], weights[rows, :]
            for a, value in enumerate((e - k * (e - d), d, k)):
                out[pl.ds(a * G8 + c * WL + w, n, stride=ARRAYS * G8), :] = value


def give(low, high, even):
    return jnp.where(even, high, low), jnp.where(even, low, high)


def take(near, far, even):
    return jnp.where(even, far, near), jnp.where(even, near, far)


def piece(got, a, g):
    n = got.shape[0] // (ARRAYS * G8)
    return got[pl.ds(a * G8 + g, n, stride=ARRAYS * G8), :]


def edge_body(got, table, near, far):
    n = near.shape[0] // ARRAYS
    even = table[5:6, :HD] > 0.5
    for a in range(ARRAYS):
        pieces = [piece(got, a, g) for g in range(G8)]
        rows = pl.ds(a * n, n)
        near[rows, :], far[rows, :] = give(pack_center(pieces, 0), pack_center(pieces, HD - OV), even)


def gram_body(got, near, far, table, x, tri):
    n = near.shape[0] // ARRAYS
    even = table[5:6, :HD] > 0.5
    keep = table[0:1, WL * HD :]
    before, after = take(near[0:n, :], far[0:n, :], even)
    for c in range(CL):
        rows = pl.ds(c * n, n)
        for w in range(WL):
            x[rows, pl.ds(w * HD, HD)] = piece(got, 0, c * WL + w)
        x[rows, pl.ds(WL * HD, HD)] = open_edges(before, after, c) * keep
    put_gram(x, tri)


def shrink_of(gram, x, factor):
    count = gram.shape[0]
    row = lax.broadcasted_iota(jnp.int32, gram.shape, 0)
    identity = (row == lanes(gram.shape)).astype(F32)
    trace = jnp.sum(jnp.sum(gram * identity, axis=1, keepdims=True), axis=0, keepdims=True)
    mean_eigen = trace / count + 1e-06
    target = (gram + (0.01 * mean_eigen) * identity) / (16.16 * mean_eigen)
    first = 1.5 * identity - 0.5 * target
    first_parts = split(first)
    target = product(split(target), first_parts)
    second = 1.5 * identity - 0.5 * product(first_parts, split(target))
    inverse_root = product(split(second), first_parts)
    return product(split(identity - factor * inverse_root), split(x))


def apply_body(step, last, tri, x, table, out, near, far, gram):
    n = x.shape[0] // CL
    even = table[5:6, :HD] > 0.5
    factor = table[3 + step : 4 + step, : gram.shape[0]]
    out[...] = shrink_of(get_gram(tri, gram), x[...], factor) * table[1:2, :]
    edges = [out[pl.ds(c * n, n), pl.ds(WL * HD, HD)] for c in range(CL)]
    near[0:n, :], far[0:n, :] = give(pack_edges(edges, 0), pack_edges(edges, WL * OV), even)
    if not last:
        pieces = [out[pl.ds(c * n, n), pl.ds(w * HD, HD)] for c in range(CL) for w in range(WL)]
        rows = slice(n, 2 * n)
        near[rows, :], far[rows, :] = give(pack_center(pieces, 0), pack_center(pieces, HD - OV), even)


def next_body(got, near, far, s, s_near, s_far, table, x, tri):
    n = near.shape[0] // ARRAYS
    even = table[5:6, :HD] > 0.5
    keep = table[0:1, WL * HD :]
    scale = table[2:3, :]
    center = take(s_near[0:n, :], s_far[0:n, :], even)
    outer = take(s_near[n : 2 * n, :], s_far[n : 2 * n, :], even)
    d_edges = take(near[n : 2 * n, :], far[n : 2 * n, :], even)
    k_edges = take(near[2 * n :, :], far[2 * n :, :], even)
    for c in range(CL):
        rows = pl.ds(c * n, n)

        def moved(total, cols, d, k):
            current = total * scale[:, cols]
            return current - k * (current - d)

        for w in range(WL):
            g = c * WL + w
            cols = slice(w * HD, w * HD + HD)
            total = s[rows, cols] + open_center(*center, g)
            x[rows, cols] = moved(total, cols, piece(got, 1, g), piece(got, 2, g))
        cols = slice(WL * HD, WL * HD + HD)
        total = s[rows, cols] + open_edges(*outer, c)
        x[rows, cols] = moved(total, cols, open_edges(*d_edges, c), open_edges(*k_edges, c)) * keep
    put_gram(x, tri)


def close_body(s, near, far, table, out):
    n = near.shape[0]
    center = take(near[...], far[...], table[5:6, :HD] > 0.5)
    for c in range(CL):
        for w in range(WL):
            g = c * WL + w
            total = s[pl.ds(c * n, n), pl.ds(w * HD, HD)] + open_center(*center, g)
            out[pl.ds(g, n, stride=G8), :] = total * table[2:3, w * HD : w * HD + HD]


def unpack_body(got, out):
    n = got.shape[0] // G8
    for c in range(CL):
        for w in range(WL):
            out[pl.ds(c * WL * n + w, n, stride=WL), :] = got[pl.ds(c * WL + w, n, stride=G8), :]


def run(body, name, shapes, *args, enter=True, leave=True, scratch=()):
    spec = pl.BlockSpec(memory_space=pltpu.VMEM)
    outs = [pltpu.VMEM(s, F32) if leave else jax.ShapeDtypeStruct(s, F32) for s in shapes]
    single = len(outs) == 1
    if enter:
        args = [pltpu.with_memory_space_constraint(a, pltpu.VMEM) for a in args]
    return pl.pallas_call(
        body,
        out_shape=outs[0] if single else outs,
        in_specs=[spec] * len(args),
        out_specs=spec if single else [spec] * len(outs),
        scratch_shapes=[pltpu.VMEM(t, F32) for t in scratch],
        name=name,
    )(*args)


def exchange(x, n):
    return lax.all_to_all(x.reshape(n, -1, HD), "chan", 0, 0).reshape(x.shape)


def swap(near, far):
    size = lax.axis_size("facet")
    apart = [(i, i + 1) for i in range(1, size - 1, 2)]
    beside = [(i, i + 1) for i in range(0, size, 2)]
    near = lax.ppermute(near, "facet", beside + [(j, i) for i, j in beside])
    far = lax.ppermute(far, "facet", apart + [(j, i) for i, j in apart])
    return near, far


def total_gram(tri, n):
    parts = tri.reshape(n, 1, -1)
    mine = jnp.sum(lax.all_to_all(parts, "chan", 0, 0), axis=0, keepdims=True)
    return lax.all_to_all(jnp.broadcast_to(mine, parts.shape), "chan", 0, 0).reshape(tri.shape)


def tables(margin, blend_table, tau_steps, channels):
    facet_id = lax.axis_index("facet")
    facet_total = lax.axis_size("facet")
    row_index = jnp.arange(HD + 2 * OV, dtype=jnp.int32)[None, :]
    keep_all = (
        (row_index >= OV - margin[:, None]) & (row_index < HD + OV + margin[:, None])
    ).astype(F32)
    weight_all = blend_table.astype(F32) * keep_all
    row_weight = weight_all[facet_id]
    before = weight_all[jnp.maximum(facet_id - 1, 0)][HD:] * (facet_id > 0)
    after = weight_all[jnp.minimum(facet_id + 1, facet_total - 1)][: 2 * OV] * (
        facet_id < facet_total - 1
    )
    total = row_weight + jnp.concatenate([before, jnp.zeros((HD - 2 * OV,), F32), after])
    scale = 1.0 / jnp.where(total == 0.0, 1.0, total)
    rows = jnp.stack([keep_all[facet_id], row_weight, scale])
    center, low, high = rows[:, OV : OV + HD], rows[:, :OV], rows[:, OV + HD :]
    pad = jnp.zeros((3, HD - 4 * OV), F32)
    rows = jnp.concatenate([center, center, low, low, high, high, pad], axis=1)
    factors = 0.1 * tau_steps.astype(F32) / math.sqrt(1.01)
    factors = jnp.broadcast_to(factors[:, None], (tau_steps.shape[0], rows.shape[1]))
    even = jnp.broadcast_to((facet_id % 2 == 0).astype(F32), (1, rows.shape[1]))
    return jnp.concatenate([rows, factors, even, jnp.zeros((2, rows.shape[1]), F32)])


def per_device(estimate, dirty, weights, margin, blend_table, tau_steps):
    n = lax.axis_size("chan")
    c, width = n * CL, (WL + 1) * HD
    assert estimate.shape == (CL, n * WL, HD)
    table = tables(margin, blend_table, tau_steps, c)
    flat = (CL * WL * n, HD)
    sent = run(
        pack_body, "pack", [(ARRAYS * G8 * n, HD)], estimate.reshape(flat), dirty.reshape(flat), weights.reshape(flat), enter=False
    )
    got = exchange(sent, n)
    near, far = swap(*run(edge_body, "edges", [(ARRAYS * n, HD)] * 2, got, table))
    sums = (n * pl.cdiv(c * (c + 1) // 2, n * HD), HD)
    x, gram = run(gram_body, "gram", [(c, width), sums], got, near, far, table)
    gram = total_gram(gram, n)
    s, s_near, s_far = run(
        lambda *refs: apply_body(0, False, *refs), "shrink", [(c, width), (2 * n, HD), (2 * n, HD)], gram, x, table, scratch=[(c, c)]
    )
    s_near, s_far = swap(s_near, s_far)
    x, gram = run(next_body, "step", [(c, width), sums], got, near, far, s, s_near, s_far, table)
    gram = total_gram(gram, n)
    s, s_near, s_far = run(
        lambda *refs: apply_body(1, True, *refs), "last", [(c, width), (n, HD), (n, HD)], gram, x, table, scratch=[(c, c)]
    )
    s_near, s_far = swap(s_near, s_far)
    back = exchange(run(close_body, "close", [(G8 * n, HD)], s, s_near, s_far, table), n)
    return run(unpack_body, "unpack", [flat], back, leave=False).reshape(estimate.shape)


def solution(mesh):
    placed = (
        P("chan", None, "facet"),
        P("chan", None, "facet"),
        P("chan", None, "facet"),
        P(),
        P(),
        P(),
    )
    return jax.shard_map(
        per_device, mesh=mesh, in_specs=placed, out_specs=P("chan", None, "facet"), check_vma=False
    )
```

time: 165 us -> 161 us (0.976)
  the two profiles are of different devices: /device:TPU:1 before, /device:TPU:17 now
where the time goes in v3:
time: 161 us; the launch traced here: 160 us
  blocking collectives  78.2 us (49%)
  starting transfers between devices  37.4 us (23%)
  waiting for transfers between devices  33.7 us (21%)
  Pallas kernels  7.97 us (5%)
  local copies, waits for them, and re-layouts  1.9 us (1%)
    all_to_all x2, blocking collectives, total_gram(): mine = jnp.sum(lax.all_to_all(parts, 'chan', 0, 0), axis=0, keepdims=True)  31.3 us
    all_to_all x2, blocking collectives, total_gram(): lax.all_to_all(jnp.broadcast_to(mine, parts.shape), 'chan', 0, 0)  29.6 us
    all_to_all x1, waiting for transfers between devices, exchange(): return lax.all_to_all(x.reshape(n, -1, HD), 'chan', 0, 0).reshape(x.shape)  20 us
    all_to_all x1, blocking collectives, exchange(): return lax.all_to_all(x.reshape(n, -1, HD), 'chan', 0, 0).reshape(x.shape)  17.3 us
    all_to_all x1, starting transfers between devices, exchange(): return lax.all_to_all(x.reshape(n, -1, HD), 'chan', 0, 0).reshape(x.shape)  14.6 us
    ppermute x3, waiting for transfers between devices, swap(): far = lax.ppermute(far, 'facet', apart + [(j, i) for i, j in apart])  13.6 us
    ppermute x3, starting transfers between devices, swap(): near = lax.ppermute(near, 'facet', beside + [(j, i) for i, j in beside])  13 us
    ppermute x3, starting transfers between devices, swap(): far = lax.ppermute(far, 'facet', apart + [(j, i) for i, j in apart])  9.76 us
  transfers between devices with their start and end apart: 7, of which 4 were waited for; matrix products, arithmetic and copies ran while one was open for 1% of the time, Pallas kernels for 0%

profile of v3, /device:TPU:17, one launch (start us, length us, event | category | flops | bytes accessed | tf_op | source)
XLA Modules:
  0.0 159.9 jit_solution(5404154778194470767)
XLA Ops:
  0.0 2.2 %pack.1 = f32[1536,128]{1,0:T(8,128)} custom-call(f32[512,128]{1,0:T(8,128)} %bitcast.23, f32[512,128]{1,0:T(8,128)} %bitcast.24, f32[512,128]{1,0:T(8,128)} %bitcast.25), custom_call_target="tpu_custom_call" | custom-call | tf_op jit(solution)/shard_map/pack/pallas_call | solution.py:222
  2.2 14.6 %all-to-all-start = ((f32[64,24,128]{2,1,0:T(8,128)}), f32[64,24,128]{2,1,0:T(8,128)S(1)}, u32[]{:S(2)}, u32[]{:S(2)}) async-start(f32[64,24,128]{2,1,0:T(8,128)} %bitcast.3), calls=%async_computation | async-start | bytes 1572864 | tf_op jit(solution)/shard_map/all_to_all | solution.py:233
  16.9 0.6 copy-done.2
  18.0 0.5 copy-done
  18.6 0.1 dynamic-slice_multiply_fusion
  18.8 0.1 concatenate.11
  19.0 20.0 %all-to-all-done = f32[64,24,128]{2,1,0:T(8,128)S(1)} async-done(((f32[64,24,128]{2,1,0:T(8,128)}), f32[64,24,128]{2,1,0:T(8,128)S(1)}, u32[]{:S(2)}, u32[]{:S(2)}) %all-to-all-start) | async-done | bytes 786464 | tf_op jit(solution)/shard_map/all_to_all | solution.py:233
  39.0 0.4 edges.1
  39.5 4.0 %collective-permute-start = (f32[192,128]{1,0:T(8,128)S(1)}, f32[192,128]{1,0:T(8,128)S(1)}, u32[]{:S(2)}, u32[]{:S(2)}) collective-permute-start(f32[192,128]{1,0:T(8,128)S(1)} %get-tuple-element.17), channel_id=1, source_target_pairs={{0,1},{2,3},{4,5},{6,7},{1,0},{3,2},{5,4},{7,6},{8,9},{10,11},{12,... | collective-permute-start | bytes 294920 | tf_op jit(solution)/shard_map/ppermute | solution.py:240
  43.4 4.4 %collective-permute-start.1 = (f32[192,128]{1,0:T(8,128)S(1)}, f32[192,128]{1,0:T(8,128)S(1)}, u32[]{:S(2)}, u32[]{:S(2)}) collective-permute-start(f32[192,128]{1,0:T(8,128)S(1)} %get-tuple-element.18), channel_id=1, source_target_pairs={{1,2},{3,4},{5,6},{2,1},{4,3},{6,5},{9,10},{11,12},{13,14},{10,9},... | collective-permute-start | bytes 294920 | tf_op jit(solution)/shard_map/ppermute | solution.py:241
  47.9 4.0 %collective-permute-done.1.far = f32[192,128]{1,0:T(8,128)S(1)} collective-permute-done((f32[192,128]{1,0:T(8,128)S(1)}, f32[192,128]{1,0:T(8,128)S(1)}, u32[]{:S(2)}, u32[]{:S(2)}) %collective-permute-start.1) | collective-permute-done | bytes 98336 | tf_op jit(solution)/shard_map/ppermute | solution.py:241
  51.8 0.6 gram.1
  52.4 17.2 %all_to_all.30 = f32[64,1,640]{2,1,0:T(1,128)S(1)} all-to-all(f32[64,1,640]{2,1,0:T(1,128)S(1)} %bitcast.22), channel_id=1, replica_groups=mesh['chan'=64,'facet'=8] {'chan'}, dimensions={0} | all-to-all | bytes 327680 | tf_op jit(solution)/shard_map/all_to_all | solution.py:247
  69.6 0.1 reduce_sum.18
  69.8 0.1 broadcast_in_dim.40
  69.9 14.0 %all_to_all.31 = f32[64,1,640]{2,1,0:T(1,128)S(1)} all-to-all(f32[64,1,640]{2,1,0:T(1,128)S(1)} %broadcast_in_dim.40), channel_id=1, replica_groups=mesh['chan'=64,'facet'=8] {'chan'}, dimensions={0} | all-to-all | bytes 327680 | tf_op jit(solution)/shard_map/all_to_all | solution.py:248
  83.9 1.6 %shrink.1 = (f32[256,384]{1,0:T(8,128)S(1)}, f32[128,128]{1,0:T(8,128)S(1)}, f32[128,128]{1,0:T(8,128)S(1)}) custom-call(f32[320,128]{1,0:T(8,128)S(1)} %bitcast.19, f32[256,384]{1,0:T(8,128)S(1)} %get-tuple-element.20.refs_1_, f32[8,384]{1,0:T(8,128)S(1)} %maximum_maximum_fusion.table.refs_2_), custom_call_target="tpu_custom_call" | custom-call | tf_op jit(solution)/shard_map/shrink/pallas_call | solution.py:222
  85.5 4.5 %collective-permute-start.2 = (f32[128,128]{1,0:T(8,128)S(1)}, f32[128,128]{1,0:T(8,128)S(1)}, u32[]{:S(2)}, u32[]{:S(2)}) collective-permute-start(f32[128,128]{1,0:T(8,128)S(1)} %get-tuple-element.22), channel_id=1, source_target_pairs={{0,1},{2,3},{4,5},{6,7},{1,0},{3,2},{5,4},{7,6},{8,9},{10,11},{12,... | collective-permute-start | bytes 196616 | tf_op jit(solution)/shard_map/ppermute | solution.py:240
  90.0 3.1 %collective-permute-start.3 = (f32[128,128]{1,0:T(8,128)S(1)}, f32[128,128]{1,0:T(8,128)S(1)}, u32[]{:S(2)}, u32[]{:S(2)}) collective-permute-start(f32[128,128]{1,0:T(8,128)S(1)} %get-tuple-element.23), channel_id=1, source_target_pairs={{1,2},{3,4},{5,6},{2,1},{4,3},{6,5},{9,10},{11,12},{13,14},{10,9},... | collective-permute-start | bytes 196616 | tf_op jit(solution)/shard_map/ppermute | solution.py:241
  93.2 4.6 %collective-permute-done.3.s_far = f32[128,128]{1,0:T(8,128)S(1)} collective-permute-done((f32[128,128]{1,0:T(8,128)S(1)}, f32[128,128]{1,0:T(8,128)S(1)}, u32[]{:S(2)}, u32[]{:S(2)}) %collective-permute-start.3) | collective-permute-done | bytes 65568 | tf_op jit(solution)/shard_map/ppermute | solution.py:241
  97.7 0.7 step.1
  98.4 14.1 %all_to_all.32 = f32[64,1,640]{2,1,0:T(1,128)S(1)} all-to-all(f32[64,1,640]{2,1,0:T(1,128)S(1)} %bitcast.21), channel_id=1, replica_groups=mesh['chan'=64,'facet'=8] {'chan'}, dimensions={0} | all-to-all | bytes 327680 | tf_op jit(solution)/shard_map/all_to_all | solution.py:247
  112.5 0.1 reduce_sum.19
  112.6 0.1 broadcast_in_dim.41
  112.7 15.6 %all_to_all.33 = f32[64,1,640]{2,1,0:T(1,128)S(1)} all-to-all(f32[64,1,640]{2,1,0:T(1,128)S(1)} %broadcast_in_dim.41), channel_id=1, replica_groups=mesh['chan'=64,'facet'=8] {'chan'}, dimensions={0} | all-to-all | bytes 327680 | tf_op jit(solution)/shard_map/all_to_all | solution.py:248
  128.3 1.5 last.1
  129.8 4.5 %collective-permute-start.4 = (f32[64,128]{1,0:T(8,128)S(1)}, f32[64,128]{1,0:T(8,128)S(1)}, u32[]{:S(2)}, u32[]{:S(2)}) collective-permute-start(f32[64,128]{1,0:T(8,128)S(1)} %get-tuple-element.27), channel_id=1, source_target_pairs={{0,1},{2,3},{4,5},{6,7},{1,0},{3,2},{5,4},{7,6},{8,9},{10,11},{12,... | collective-permute-start | bytes 98312 | tf_op jit(solution)/shard_map/ppermute | solution.py:240
  134.3 2.2 %collective-permute-start.5 = (f32[64,128]{1,0:T(8,128)S(1)}, f32[64,128]{1,0:T(8,128)S(1)}, u32[]{:S(2)}, u32[]{:S(2)}) collective-permute-start(f32[64,128]{1,0:T(8,128)S(1)} %get-tuple-element.28), channel_id=1, source_target_pairs={{1,2},{3,4},{5,6},{2,1},{4,3},{6,5},{9,10},{11,12},{13,14},{10,9},... | collective-permute-start | bytes 98312 | tf_op jit(solution)/shard_map/ppermute | solution.py:241
  136.5 5.1 %collective-permute-done.5.far = f32[64,128]{1,0:T(8,128)S(1)} collective-permute-done((f32[64,128]{1,0:T(8,128)S(1)}, f32[64,128]{1,0:T(8,128)S(1)}, u32[]{:S(2)}, u32[]{:S(2)}) %collective-permute-start.5) | collective-permute-done | bytes 32800 | tf_op jit(solution)/shard_map/ppermute | solution.py:241
  141.6 0.2 close.1
  141.8 17.3 %all_to_all.34 = f32[64,8,128]{2,1,0:T(8,128)S(1)} all-to-all(f32[64,8,128]{2,1,0:T(8,128)S(1)} %bitcast.18), channel_id=1, replica_groups=mesh['chan'=64,'facet'=8] {'chan'}, dimensions={0} | all-to-all | bytes 524288 | tf_op jit(solution)/shard_map/all_to_all | solution.py:233
  159.1 0.8 unpack.1
  (24 shorter events, 0.7 us)
Async XLA Ops:
  2.2 14.7 %copy-start.1 = (s32[8]{0:T(128)S(1)}, s32[8]{0:T(128)}, u32[]{:S(2)}) copy-start(s32[8]{0:T(128)} %param.9) | copy-start | bytes 100
  2.2 36.8 %all-to-all-start = ((f32[64,24,128]{2,1,0:T(8,128)}), f32[64,24,128]{2,1,0:T(8,128)S(1)}, u32[]{:S(2)}, u32[]{:S(2)}) async-start(f32[64,24,128]{2,1,0:T(8,128)} %bitcast.3), calls=%async_computation | async-start | bytes 1572864 | tf_op jit(solution)/shard_map/all_to_all | solution.py:233
  16.9 0.7 copy-start.2
  17.8 0.7 copy-start
  39.5 8.4 %collective-permute-start = (f32[192,128]{1,0:T(8,128)S(1)}, f32[192,128]{1,0:T(8,128)S(1)}, u32[]{:S(2)}, u32[]{:S(2)}) collective-permute-start(f32[192,128]{1,0:T(8,128)S(1)} %get-tuple-element.17), channel_id=1, source_target_pairs={{0,1},{2,3},{4,5},{6,7},{1,0},{3,2},{5,4},{7,6},{8,9},{10,11},{12,... | collective-permute-start | bytes 294920 | tf_op jit(solution)/shard_map/ppermute | solution.py:240
  43.4 8.4 %collective-permute-start.1 = (f32[192,128]{1,0:T(8,128)S(1)}, f32[192,128]{1,0:T(8,128)S(1)}, u32[]{:S(2)}, u32[]{:S(2)}) collective-permute-start(f32[192,128]{1,0:T(8,128)S(1)} %get-tuple-element.18), channel_id=1, source_target_pairs={{1,2},{3,4},{5,6},{2,1},{4,3},{6,5},{9,10},{11,12},{13,14},{10,9},... | collective-permute-start | bytes 294920 | tf_op jit(solution)/shard_map/ppermute | solution.py:241
  85.5 7.7 %collective-permute-start.2 = (f32[128,128]{1,0:T(8,128)S(1)}, f32[128,128]{1,0:T(8,128)S(1)}, u32[]{:S(2)}, u32[]{:S(2)}) collective-permute-start(f32[128,128]{1,0:T(8,128)S(1)} %get-tuple-element.22), channel_id=1, source_target_pairs={{0,1},{2,3},{4,5},{6,7},{1,0},{3,2},{5,4},{7,6},{8,9},{10,11},{12,... | collective-permute-start | bytes 196616 | tf_op jit(solution)/shard_map/ppermute | solution.py:240
  90.0 7.7 %collective-permute-start.3 = (f32[128,128]{1,0:T(8,128)S(1)}, f32[128,128]{1,0:T(8,128)S(1)}, u32[]{:S(2)}, u32[]{:S(2)}) collective-permute-start(f32[128,128]{1,0:T(8,128)S(1)} %get-tuple-element.23), channel_id=1, source_target_pairs={{1,2},{3,4},{5,6},{2,1},{4,3},{6,5},{9,10},{11,12},{13,14},{10,9},... | collective-permute-start | bytes 196616 | tf_op jit(solution)/shard_map/ppermute | solution.py:241
  129.8 6.7 %collective-permute-start.4 = (f32[64,128]{1,0:T(8,128)S(1)}, f32[64,128]{1,0:T(8,128)S(1)}, u32[]{:S(2)}, u32[]{:S(2)}) collective-permute-start(f32[64,128]{1,0:T(8,128)S(1)} %get-tuple-element.27), channel_id=1, source_target_pairs={{0,1},{2,3},{4,5},{6,7},{1,0},{3,2},{5,4},{7,6},{8,9},{10,11},{12,... | collective-permute-start | bytes 98312 | tf_op jit(solution)/shard_map/ppermute | solution.py:240
  134.3 7.3 %collective-permute-start.5 = (f32[64,128]{1,0:T(8,128)S(1)}, f32[64,128]{1,0:T(8,128)S(1)}, u32[]{:S(2)}, u32[]{:S(2)}) collective-permute-start(f32[64,128]{1,0:T(8,128)S(1)} %get-tuple-element.28), channel_id=1, source_target_pairs={{1,2},{3,4},{5,6},{2,1},{4,3},{6,5},{9,10},{11,12},{13,14},{10,9},... | collective-permute-start | bytes 98312 | tf_op jit(solution)/shard_map/ppermute | solution.py:241

commit v4 on v3

--- a/solution.py
+++ b/solution.py
@@ -213,7 +213,7 @@
             out[pl.ds(c * WL * n + w, n, stride=WL), :] = got[pl.ds(c * WL + w, n, stride=G8), :]
 
 
-def run(body, name, shapes, *args, enter=True, leave=True, scratch=()):
+def run(body, shapes, *args, enter=True, leave=True, scratch=()):
     spec = pl.BlockSpec(memory_space=pltpu.VMEM)
     outs = [pltpu.VMEM(s, F32) if leave else jax.ShapeDtypeStruct(s, F32) for s in shapes]
     single = len(outs) == 1
@@ -225,7 +225,6 @@
         in_specs=[spec] * len(args),
         out_specs=spec if single else [spec] * len(outs),
         scratch_shapes=[pltpu.VMEM(t, F32) for t in scratch],
-        name=name,
     )(*args)
 
 
@@ -248,7 +247,7 @@
     return lax.all_to_all(jnp.broadcast_to(mine, parts.shape), "chan", 0, 0).reshape(tri.shape)
 
 
-def tables(margin, blend_table, tau_steps, channels):
+def tables(margin, blend_table, tau_steps):
     facet_id = lax.axis_index("facet")
     facet_total = lax.axis_size("facet")
     row_index = jnp.arange(HD + 2 * OV, dtype=jnp.int32)[None, :]
@@ -277,28 +276,28 @@
     n = lax.axis_size("chan")
     c, width = n * CL, (WL + 1) * HD
     assert estimate.shape == (CL, n * WL, HD)
-    table = tables(margin, blend_table, tau_steps, c)
+    table = tables(margin, blend_table, tau_steps)
     flat = (CL * WL * n, HD)
     sent = run(
-        pack_body, "pack", [(ARRAYS * G8 * n, HD)], estimate.reshape(flat), dirty.reshape(flat), weights.reshape(flat), enter=False
+        pack_body, [(ARRAYS * G8 * n, HD)], estimate.reshape(flat), dirty.reshape(flat), weights.reshape(flat), enter=False
     )
     got = exchange(sent, n)
-    near, far = swap(*run(edge_body, "edges", [(ARRAYS * n, HD)] * 2, got, table))
+    near, far = swap(*run(edge_body, [(ARRAYS * n, HD)] * 2, got, table))
     sums = (n * pl.cdiv(c * (c + 1) // 2, n * HD), HD)
-    x, gram = run(gram_body, "gram", [(c, width), sums], got, near, far, table)
+    x, gram = run(gram_body, [(c, width), sums], got, near, far, table)
     gram = total_gram(gram, n)
     s, s_near, s_far = run(
-        lambda *refs: apply_body(0, False, *refs), "shrink", [(c, width), (2 * n, HD), (2 * n, HD)], gram, x, table, scratch=[(c, c)]
+        lambda *refs: apply_body(0, False, *refs), [(c, width), (2 * n, HD), (2 * n, HD)], gram, x, table, scratch=[(c, c)]
     )
     s_near, s_far = swap(s_near, s_far)
-    x, gram = run(next_body, "step", [(c, width), sums], got, near, far, s, s_near, s_far, table)
+    x, gram = run(next_body, [(c, width), sums], got, near, far, s, s_near, s_far, table)
     gram = total_gram(gram, n)
     s, s_near, s_far = run(
-        lambda *refs: apply_body(1, True, *refs), "last", [(c, width), (n, HD), (n, HD)], gram, x, table, scratch=[(c, c)]
+        lambda *refs: apply_body(1, True, *refs), [(c, width), (n, HD), (n, HD)], gram, x, table, scratch=[(c, c)]
     )
     s_near, s_far = swap(s_near, s_far)
-    back = exchange(run(close_body, "close", [(G8 * n, HD)], s, s_near, s_far, table), n)
-    return run(unpack_body, "unpack", [flat], back, leave=False).reshape(estimate.shape)
+    back = exchange(run(close_body, [(G8 * n, HD)], s, s_near, s_far, table), n)
+    return run(unpack_body, [flat], back, leave=False).reshape(estimate.shape)
 
 
 def solution(mesh):
@@ -310,6 +309,5 @@
         P(),
         P(),
     )
-    return jax.shard_map(
-        per_device, mesh=mesh, in_specs=placed, out_specs=P("chan", None, "facet"), check_vma=False
-    )
+
+    return jax.shard_map(per_device, mesh=mesh, in_specs=placed, out_specs=P("chan", None, "facet"), check_vma=False)

time: 161 us -> 161 us (level)
  no operation moved by 1% of the time
where the time goes in v4:
time: 161 us; the launch traced here: 160 us
  blocking collectives  78.2 us (49%)
  starting transfers between devices  37.4 us (23%)
  waiting for transfers between devices  33.7 us (21%)
  Pallas kernels  7.97 us (5%)
  local copies, waits for them, and re-layouts  1.9 us (1%)
    all_to_all x2, blocking collectives, total_gram(): mine = jnp.sum(lax.all_to_all(parts, 'chan', 0, 0), axis=0, keepdims=True)  31.3 us
    all_to_all x2, blocking collectives, total_gram(): lax.all_to_all(jnp.broadcast_to(mine, parts.shape), 'chan', 0, 0)  29.6 us
    all_to_all x1, waiting for transfers between devices, exchange(): return lax.all_to_all(x.reshape(n, -1, HD), 'chan', 0, 0).reshape(x.shape)  20 us
    all_to_all x1, blocking collectives, exchange(): return lax.all_to_all(x.reshape(n, -1, HD), 'chan', 0, 0).reshape(x.shape)  17.3 us
    all_to_all x1, starting transfers between devices, exchange(): return lax.all_to_all(x.reshape(n, -1, HD), 'chan', 0, 0).reshape(x.shape)  14.6 us
    ppermute x3, waiting for transfers between devices, swap(): far = lax.ppermute(far, 'facet', apart + [(j, i) for i, j in apart])  13.6 us
    ppermute x3, starting transfers between devices, swap(): near = lax.ppermute(near, 'facet', beside + [(j, i) for i, j in beside])  13 us
    ppermute x3, starting transfers between devices, swap(): far = lax.ppermute(far, 'facet', apart + [(j, i) for i, j in apart])  9.76 us
  transfers between devices with their start and end apart: 7, of which 4 were waited for; matrix products, arithmetic and copies ran while one was open for 1% of the time, Pallas kernels for 0%

profile of v4, /device:TPU:17, one launch (start us, length us, event | category | flops | bytes accessed | tf_op | source)
XLA Modules:
  0.0 159.9 jit_solution(5404154778194470767)
XLA Ops:
  0.0 2.2 %shard_map.64 = f32[1536,128]{1,0:T(8,128)} custom-call(f32[512,128]{1,0:T(8,128)} %bitcast.23, f32[512,128]{1,0:T(8,128)} %bitcast.24, f32[512,128]{1,0:T(8,128)} %bitcast.25), custom_call_target="tpu_custom_call" | custom-call | tf_op jit(solution)/shard_map/pallas_call | solution.py:222
  2.2 14.6 %all-to-all-start = ((f32[64,24,128]{2,1,0:T(8,128)}), f32[64,24,128]{2,1,0:T(8,128)S(1)}, u32[]{:S(2)}, u32[]{:S(2)}) async-start(f32[64,24,128]{2,1,0:T(8,128)} %bitcast.3), calls=%async_computation | async-start | bytes 1572864 | tf_op jit(solution)/shard_map/all_to_all | solution.py:232
  16.9 0.6 copy-done.2
  18.0 0.5 copy-done
  18.6 0.1 dynamic-slice_multiply_fusion
  18.8 0.1 concatenate.11
  19.0 20.0 %all-to-all-done = f32[64,24,128]{2,1,0:T(8,128)S(1)} async-done(((f32[64,24,128]{2,1,0:T(8,128)}), f32[64,24,128]{2,1,0:T(8,128)S(1)}, u32[]{:S(2)}, u32[]{:S(2)}) %all-to-all-start) | async-done | bytes 786464 | tf_op jit(solution)/shard_map/all_to_all | solution.py:232
  39.0 0.4 shard_map.65
  39.5 4.0 %collective-permute-start = (f32[192,128]{1,0:T(8,128)S(1)}, f32[192,128]{1,0:T(8,128)S(1)}, u32[]{:S(2)}, u32[]{:S(2)}) collective-permute-start(f32[192,128]{1,0:T(8,128)S(1)} %get-tuple-element.17), channel_id=1, source_target_pairs={{0,1},{2,3},{4,5},{6,7},{1,0},{3,2},{5,4},{7,6},{8,9},{10,11},{12,... | collective-permute-start | bytes 294920 | tf_op jit(solution)/shard_map/ppermute | solution.py:239
  43.4 4.4 %collective-permute-start.1 = (f32[192,128]{1,0:T(8,128)S(1)}, f32[192,128]{1,0:T(8,128)S(1)}, u32[]{:S(2)}, u32[]{:S(2)}) collective-permute-start(f32[192,128]{1,0:T(8,128)S(1)} %get-tuple-element.18), channel_id=1, source_target_pairs={{1,2},{3,4},{5,6},{2,1},{4,3},{6,5},{9,10},{11,12},{13,14},{10,9},... | collective-permute-start | bytes 294920 | tf_op jit(solution)/shard_map/ppermute | solution.py:240
  47.9 4.0 %collective-permute-done.1.far = f32[192,128]{1,0:T(8,128)S(1)} collective-permute-done((f32[192,128]{1,0:T(8,128)S(1)}, f32[192,128]{1,0:T(8,128)S(1)}, u32[]{:S(2)}, u32[]{:S(2)}) %collective-permute-start.1) | collective-permute-done | bytes 98336 | tf_op jit(solution)/shard_map/ppermute | solution.py:240
  51.8 0.6 shard_map.66
  52.4 17.2 %all_to_all.30 = f32[64,1,640]{2,1,0:T(1,128)S(1)} all-to-all(f32[64,1,640]{2,1,0:T(1,128)S(1)} %bitcast.22), channel_id=1, replica_groups=mesh['chan'=64,'facet'=8] {'chan'}, dimensions={0} | all-to-all | bytes 327680 | tf_op jit(solution)/shard_map/all_to_all | solution.py:246
  69.6 0.1 reduce_sum.18
  69.8 0.1 broadcast_in_dim.40
  69.9 14.0 %all_to_all.31 = f32[64,1,640]{2,1,0:T(1,128)S(1)} all-to-all(f32[64,1,640]{2,1,0:T(1,128)S(1)} %broadcast_in_dim.40), channel_id=1, replica_groups=mesh['chan'=64,'facet'=8] {'chan'}, dimensions={0} | all-to-all | bytes 327680 | tf_op jit(solution)/shard_map/all_to_all | solution.py:247
  83.9 1.6 %shard_map.67 = (f32[256,384]{1,0:T(8,128)S(1)}, f32[128,128]{1,0:T(8,128)S(1)}, f32[128,128]{1,0:T(8,128)S(1)}) custom-call(f32[320,128]{1,0:T(8,128)S(1)} %bitcast.19, f32[256,384]{1,0:T(8,128)S(1)} %get-tuple-element.20.refs_1_, f32[8,384]{1,0:T(8,128)S(1)} %maximum_maximum_fusion.table.refs_2_), custom_call_target="tpu_custom_call" | custom-call | tf_op jit(solution)/shard_map/pallas_call | solution.py:222
  85.5 4.5 %collective-permute-start.2 = (f32[128,128]{1,0:T(8,128)S(1)}, f32[128,128]{1,0:T(8,128)S(1)}, u32[]{:S(2)}, u32[]{:S(2)}) collective-permute-start(f32[128,128]{1,0:T(8,128)S(1)} %get-tuple-element.22), channel_id=1, source_target_pairs={{0,1},{2,3},{4,5},{6,7},{1,0},{3,2},{5,4},{7,6},{8,9},{10,11},{12,... | collective-permute-start | bytes 196616 | tf_op jit(solution)/shard_map/ppermute | solution.py:239
  90.0 3.1 %collective-permute-start.3 = (f32[128,128]{1,0:T(8,128)S(1)}, f32[128,128]{1,0:T(8,128)S(1)}, u32[]{:S(2)}, u32[]{:S(2)}) collective-permute-start(f32[128,128]{1,0:T(8,128)S(1)} %get-tuple-element.23), channel_id=1, source_target_pairs={{1,2},{3,4},{5,6},{2,1},{4,3},{6,5},{9,10},{11,12},{13,14},{10,9},... | collective-permute-start | bytes 196616 | tf_op jit(solution)/shard_map/ppermute | solution.py:240
  93.2 4.6 %collective-permute-done.3.s_far = f32[128,128]{1,0:T(8,128)S(1)} collective-permute-done((f32[128,128]{1,0:T(8,128)S(1)}, f32[128,128]{1,0:T(8,128)S(1)}, u32[]{:S(2)}, u32[]{:S(2)}) %collective-permute-start.3) | collective-permute-done | bytes 65568 | tf_op jit(solution)/shard_map/ppermute | solution.py:240
  97.7 0.7 shard_map.68
  98.4 14.1 %all_to_all.32 = f32[64,1,640]{2,1,0:T(1,128)S(1)} all-to-all(f32[64,1,640]{2,1,0:T(1,128)S(1)} %bitcast.21), channel_id=1, replica_groups=mesh['chan'=64,'facet'=8] {'chan'}, dimensions={0} | all-to-all | bytes 327680 | tf_op jit(solution)/shard_map/all_to_all | solution.py:246
  112.5 0.1 reduce_sum.19
  112.6 0.1 broadcast_in_dim.41
  112.7 15.6 %all_to_all.33 = f32[64,1,640]{2,1,0:T(1,128)S(1)} all-to-all(f32[64,1,640]{2,1,0:T(1,128)S(1)} %broadcast_in_dim.41), channel_id=1, replica_groups=mesh['chan'=64,'facet'=8] {'chan'}, dimensions={0} | all-to-all | bytes 327680 | tf_op jit(solution)/shard_map/all_to_all | solution.py:247
  128.3 1.5 shard_map.69
  129.8 4.5 %collective-permute-start.4 = (f32[64,128]{1,0:T(8,128)S(1)}, f32[64,128]{1,0:T(8,128)S(1)}, u32[]{:S(2)}, u32[]{:S(2)}) collective-permute-start(f32[64,128]{1,0:T(8,128)S(1)} %get-tuple-element.27), channel_id=1, source_target_pairs={{0,1},{2,3},{4,5},{6,7},{1,0},{3,2},{5,4},{7,6},{8,9},{10,11},{12,... | collective-permute-start | bytes 98312 | tf_op jit(solution)/shard_map/ppermute | solution.py:239
  134.3 2.2 %collective-permute-start.5 = (f32[64,128]{1,0:T(8,128)S(1)}, f32[64,128]{1,0:T(8,128)S(1)}, u32[]{:S(2)}, u32[]{:S(2)}) collective-permute-start(f32[64,128]{1,0:T(8,128)S(1)} %get-tuple-element.28), channel_id=1, source_target_pairs={{1,2},{3,4},{5,6},{2,1},{4,3},{6,5},{9,10},{11,12},{13,14},{10,9},... | collective-permute-start | bytes 98312 | tf_op jit(solution)/shard_map/ppermute | solution.py:240
  136.5 5.1 %collective-permute-done.5.far = f32[64,128]{1,0:T(8,128)S(1)} collective-permute-done((f32[64,128]{1,0:T(8,128)S(1)}, f32[64,128]{1,0:T(8,128)S(1)}, u32[]{:S(2)}, u32[]{:S(2)}) %collective-permute-start.5) | collective-permute-done | bytes 32800 | tf_op jit(solution)/shard_map/ppermute | solution.py:240
  141.6 0.2 shard_map.70
  141.8 17.3 %all_to_all.34 = f32[64,8,128]{2,1,0:T(8,128)S(1)} all-to-all(f32[64,8,128]{2,1,0:T(8,128)S(1)} %bitcast.18), channel_id=1, replica_groups=mesh['chan'=64,'facet'=8] {'chan'}, dimensions={0} | all-to-all | bytes 524288 | tf_op jit(solution)/shard_map/all_to_all | solution.py:232
  159.1 0.8 shard_map.71
  (24 shorter events, 0.7 us)
Async XLA Ops:
  2.2 14.7 %copy-start.1 = (s32[8]{0:T(128)S(1)}, s32[8]{0:T(128)}, u32[]{:S(2)}) copy-start(s32[8]{0:T(128)} %param.9) | copy-start | bytes 100
  2.2 36.8 %all-to-all-start = ((f32[64,24,128]{2,1,0:T(8,128)}), f32[64,24,128]{2,1,0:T(8,128)S(1)}, u32[]{:S(2)}, u32[]{:S(2)}) async-start(f32[64,24,128]{2,1,0:T(8,128)} %bitcast.3), calls=%async_computation | async-start | bytes 1572864 | tf_op jit(solution)/shard_map/all_to_all | solution.py:232
  16.9 0.7 copy-start.2
  17.8 0.7 copy-start
  39.5 8.4 %collective-permute-start = (f32[192,128]{1,0:T(8,128)S(1)}, f32[192,128]{1,0:T(8,128)S(1)}, u32[]{:S(2)}, u32[]{:S(2)}) collective-permute-start(f32[192,128]{1,0:T(8,128)S(1)} %get-tuple-element.17), channel_id=1, source_target_pairs={{0,1},{2,3},{4,5},{6,7},{1,0},{3,2},{5,4},{7,6},{8,9},{10,11},{12,... | collective-permute-start | bytes 294920 | tf_op jit(solution)/shard_map/ppermute | solution.py:239
  43.4 8.4 %collective-permute-start.1 = (f32[192,128]{1,0:T(8,128)S(1)}, f32[192,128]{1,0:T(8,128)S(1)}, u32[]{:S(2)}, u32[]{:S(2)}) collective-permute-start(f32[192,128]{1,0:T(8,128)S(1)} %get-tuple-element.18), channel_id=1, source_target_pairs={{1,2},{3,4},{5,6},{2,1},{4,3},{6,5},{9,10},{11,12},{13,14},{10,9},... | collective-permute-start | bytes 294920 | tf_op jit(solution)/shard_map/ppermute | solution.py:240
  85.5 7.7 %collective-permute-start.2 = (f32[128,128]{1,0:T(8,128)S(1)}, f32[128,128]{1,0:T(8,128)S(1)}, u32[]{:S(2)}, u32[]{:S(2)}) collective-permute-start(f32[128,128]{1,0:T(8,128)S(1)} %get-tuple-element.22), channel_id=1, source_target_pairs={{0,1},{2,3},{4,5},{6,7},{1,0},{3,2},{5,4},{7,6},{8,9},{10,11},{12,... | collective-permute-start | bytes 196616 | tf_op jit(solution)/shard_map/ppermute | solution.py:239
  90.0 7.7 %collective-permute-start.3 = (f32[128,128]{1,0:T(8,128)S(1)}, f32[128,128]{1,0:T(8,128)S(1)}, u32[]{:S(2)}, u32[]{:S(2)}) collective-permute-start(f32[128,128]{1,0:T(8,128)S(1)} %get-tuple-element.23), channel_id=1, source_target_pairs={{1,2},{3,4},{5,6},{2,1},{4,3},{6,5},{9,10},{11,12},{13,14},{10,9},... | collective-permute-start | bytes 196616 | tf_op jit(solution)/shard_map/ppermute | solution.py:240
  129.8 6.7 %collective-permute-start.4 = (f32[64,128]{1,0:T(8,128)S(1)}, f32[64,128]{1,0:T(8,128)S(1)}, u32[]{:S(2)}, u32[]{:S(2)}) collective-permute-start(f32[64,128]{1,0:T(8,128)S(1)} %get-tuple-element.27), channel_id=1, source_target_pairs={{0,1},{2,3},{4,5},{6,7},{1,0},{3,2},{5,4},{7,6},{8,9},{10,11},{12,... | collective-permute-start | bytes 98312 | tf_op jit(solution)/shard_map/ppermute | solution.py:239
  134.3 7.3 %collective-permute-start.5 = (f32[64,128]{1,0:T(8,128)S(1)}, f32[64,128]{1,0:T(8,128)S(1)}, u32[]{:S(2)}, u32[]{:S(2)}) collective-permute-start(f32[64,128]{1,0:T(8,128)S(1)} %get-tuple-element.28), channel_id=1, source_target_pairs={{1,2},{3,4},{5,6},{2,1},{4,3},{6,5},{9,10},{11,12},{13,14},{10,9},... | collective-permute-start | bytes 98312 | tf_op jit(solution)/shard_map/ppermute | solution.py:240

commit v5 on v4

--- a/solution.py
+++ b/solution.py
@@ -106,11 +106,17 @@
                 out[pl.ds(a * G8 + c * WL + w, n, stride=ARRAYS * G8), :] = value
 
 
-def give(low, high, even):
+def is_even():
+    return lax.axis_index("facet") % 2 == 0
+
+
+def give(low, high):
+    even = is_even()
     return jnp.where(even, high, low), jnp.where(even, low, high)
 
 
-def take(near, far, even):
+def take(near, far):
+    even = is_even()
     return jnp.where(even, far, near), jnp.where(even, near, far)
 
 
@@ -119,20 +125,18 @@
     return got[pl.ds(a * G8 + g, n, stride=ARRAYS * G8), :]
 
 
-def edge_body(got, table, near, far):
-    n = near.shape[0] // ARRAYS
-    even = table[5:6, :HD] > 0.5
-    for a in range(ARRAYS):
+def edge_body(got, near, far):
+    n = near.shape[0] // 2
+    for i, a in enumerate((0, 2)):
         pieces = [piece(got, a, g) for g in range(G8)]
-        rows = pl.ds(a * n, n)
-        near[rows, :], far[rows, :] = give(pack_center(pieces, 0), pack_center(pieces, HD - OV), even)
+        rows = pl.ds(i * n, n)
+        near[rows, :], far[rows, :] = give(pack_center(pieces, 0), pack_center(pieces, HD - OV))
 
 
 def gram_body(got, near, far, table, x, tri):
-    n = near.shape[0] // ARRAYS
-    even = table[5:6, :HD] > 0.5
+    n = near.shape[0] // 2
     keep = table[0:1, WL * HD :]
-    before, after = take(near[0:n, :], far[0:n, :], even)
+    before, after = take(near[0:n, :], far[0:n, :])
     for c in range(CL):
         rows = pl.ds(c * n, n)
         for w in range(WL):
@@ -149,56 +153,59 @@
     mean_eigen = trace / count + 1e-06
     target = (gram + (0.01 * mean_eigen) * identity) / (16.16 * mean_eigen)
     first = 1.5 * identity - 0.5 * target
-    first_parts = split(first)
-    target = product(split(target), first_parts)
-    second = 1.5 * identity - 0.5 * product(first_parts, split(target))
-    inverse_root = product(split(second), first_parts)
+    parts = split(target)
+    square = product(parts, parts)
+    stepped = 1.5 * target - 0.5 * square
+    twice = 2.25 * identity - 1.5 * target + 0.25 * square
+    inverse_root = 1.5 * first - 0.5 * product(split(stepped), split(twice))
     return product(split(identity - factor * inverse_root), split(x))
 
 
-def apply_body(step, last, tri, x, table, out, near, far, gram):
+def apply_body(step, tri, x, table, out, near, far, gram):
     n = x.shape[0] // CL
-    even = table[5:6, :HD] > 0.5
     factor = table[3 + step : 4 + step, : gram.shape[0]]
     out[...] = shrink_of(get_gram(tri, gram), x[...], factor) * table[1:2, :]
     edges = [out[pl.ds(c * n, n), pl.ds(WL * HD, HD)] for c in range(CL)]
-    near[0:n, :], far[0:n, :] = give(pack_edges(edges, 0), pack_edges(edges, WL * OV), even)
-    if not last:
-        pieces = [out[pl.ds(c * n, n), pl.ds(w * HD, HD)] for c in range(CL) for w in range(WL)]
-        rows = slice(n, 2 * n)
-        near[rows, :], far[rows, :] = give(pack_center(pieces, 0), pack_center(pieces, HD - OV), even)
+    near[0:n, :], far[0:n, :] = give(pack_edges(edges, 0), pack_edges(edges, WL * OV))
+
+
+def zone_body(tri, x, got, table, out, near, far, gram):
+    apply_body(0, tri, x, table, out, near, far, gram)
+    n = x.shape[0] // CL
+    pieces = []
+    for g in range(G8):
+        cols = pl.ds(g % WL * HD, HD)
+        d, k = piece(got, 1, g), piece(got, 2, g)
+        own = out[pl.ds(g // WL * n, n), cols] * table[2:3, :HD]
+        pieces.append(own - k * (own - d))
+    rows = slice(n, 2 * n)
+    near[rows, :], far[rows, :] = give(pack_center(pieces, 0), pack_center(pieces, HD - OV))
 
 
 def next_body(got, near, far, s, s_near, s_far, table, x, tri):
-    n = near.shape[0] // ARRAYS
-    even = table[5:6, :HD] > 0.5
+    n = near.shape[0] // 2
     keep = table[0:1, WL * HD :]
     scale = table[2:3, :]
-    center = take(s_near[0:n, :], s_far[0:n, :], even)
-    outer = take(s_near[n : 2 * n, :], s_far[n : 2 * n, :], even)
-    d_edges = take(near[n : 2 * n, :], far[n : 2 * n, :], even)
-    k_edges = take(near[2 * n :, :], far[2 * n :, :], even)
+    center = take(s_near[0:n, :], s_far[0:n, :])
+    outer = take(s_near[n : 2 * n, :], s_far[n : 2 * n, :])
+    k_edges = take(near[n : 2 * n, :], far[n : 2 * n, :])
     for c in range(CL):
         rows = pl.ds(c * n, n)
-
-        def moved(total, cols, d, k):
-            current = total * scale[:, cols]
-            return current - k * (current - d)
-
         for w in range(WL):
             g = c * WL + w
             cols = slice(w * HD, w * HD + HD)
-            total = s[rows, cols] + open_center(*center, g)
-            x[rows, cols] = moved(total, cols, piece(got, 1, g), piece(got, 2, g))
+            d, k = piece(got, 1, g), piece(got, 2, g)
+            current = (s[rows, cols] + open_center(*center, g)) * scale[:, cols]
+            x[rows, cols] = current - k * (current - d)
         cols = slice(WL * HD, WL * HD + HD)
-        total = s[rows, cols] + open_edges(*outer, c)
-        x[rows, cols] = moved(total, cols, open_edges(*d_edges, c), open_edges(*k_edges, c)) * keep
+        own = s[rows, cols] * scale[:, cols]
+        x[rows, cols] = (own - open_edges(*k_edges, c) * own + open_edges(*outer, c)) * keep
     put_gram(x, tri)
 
 
 def close_body(s, near, far, table, out):
     n = near.shape[0]
-    center = take(near[...], far[...], table[5:6, :HD] > 0.5)
+    center = take(near[...], far[...])
     for c in range(CL):
         for w in range(WL):
             g = c * WL + w
@@ -256,44 +263,49 @@
     ).astype(F32)
     weight_all = blend_table.astype(F32) * keep_all
     row_weight = weight_all[facet_id]
-    before = weight_all[jnp.maximum(facet_id - 1, 0)][HD:] * (facet_id > 0)
-    after = weight_all[jnp.minimum(facet_id + 1, facet_total - 1)][: 2 * OV] * (
+    before = weight_all[:, HD:][jnp.maximum(facet_id - 1, 0)] * (facet_id > 0)
+    after = weight_all[:, : 2 * OV][jnp.minimum(facet_id + 1, facet_total - 1)] * (
         facet_id < facet_total - 1
     )
-    total = row_weight + jnp.concatenate([before, jnp.zeros((HD - 2 * OV,), F32), after])
+    total = row_weight + jnp.pad(before, (0, HD)) + jnp.pad(after, (HD, 0))
     scale = 1.0 / jnp.where(total == 0.0, 1.0, total)
     rows = jnp.stack([keep_all[facet_id], row_weight, scale])
     center, low, high = rows[:, OV : OV + HD], rows[:, :OV], rows[:, OV + HD :]
-    pad = jnp.zeros((3, HD - 4 * OV), F32)
-    rows = jnp.concatenate([center, center, low, low, high, high, pad], axis=1)
+    rows = jnp.concatenate([center, center, low, low, high, high], axis=1)
+    rows = jnp.pad(rows, ((0, 5), (0, HD - 4 * OV)))
     factors = 0.1 * tau_steps.astype(F32) / math.sqrt(1.01)
-    factors = jnp.broadcast_to(factors[:, None], (tau_steps.shape[0], rows.shape[1]))
-    even = jnp.broadcast_to((facet_id % 2 == 0).astype(F32), (1, rows.shape[1]))
-    return jnp.concatenate([rows, factors, even, jnp.zeros((2, rows.shape[1]), F32)])
+    return rows + jnp.pad(factors, (3, 5 - tau_steps.shape[0]))[:, None]
 
 
 def per_device(estimate, dirty, weights, margin, blend_table, tau_steps):
     n = lax.axis_size("chan")
     c, width = n * CL, (WL + 1) * HD
     assert estimate.shape == (CL, n * WL, HD)
-    table = tables(margin, blend_table, tau_steps)
     flat = (CL * WL * n, HD)
     sent = run(
-        pack_body, [(ARRAYS * G8 * n, HD)], estimate.reshape(flat), dirty.reshape(flat), weights.reshape(flat), enter=False
+        pack_body,
+        [(ARRAYS * G8 * n, HD)],
+        estimate.reshape(flat),
+        dirty.reshape(flat),
+        weights.reshape(flat),
+        enter=False,
     )
     got = exchange(sent, n)
-    near, far = swap(*run(edge_body, [(ARRAYS * n, HD)] * 2, got, table))
+    near, far = run(edge_body, [(2 * n, HD)] * 2, got)
+    near, far, *small = lax.optimization_barrier((near, far, margin, blend_table, tau_steps))
+    near, far = swap(near, far)
+    table = tables(*small)
     sums = (n * pl.cdiv(c * (c + 1) // 2, n * HD), HD)
     x, gram = run(gram_body, [(c, width), sums], got, near, far, table)
     gram = total_gram(gram, n)
     s, s_near, s_far = run(
-        lambda *refs: apply_body(0, False, *refs), [(c, width), (2 * n, HD), (2 * n, HD)], gram, x, table, scratch=[(c, c)]
+        zone_body, [(c, width), (2 * n, HD), (2 * n, HD)], gram, x, got, table, scratch=[(c, c)]
     )
     s_near, s_far = swap(s_near, s_far)
     x, gram = run(next_body, [(c, width), sums], got, near, far, s, s_near, s_far, table)
     gram = total_gram(gram, n)
     s, s_near, s_far = run(
-        lambda *refs: apply_body(1, True, *refs), [(c, width), (n, HD), (n, HD)], gram, x, table, scratch=[(c, c)]
+        lambda *refs: apply_body(1, *refs), [(c, width), (n, HD), (n, HD)], gram, x, table, scratch=[(c, c)]
     )
     s_near, s_far = swap(s_near, s_far)
     back = exchange(run(close_body, [(G8 * n, HD)], s, s_near, s_far, table), n)

time: 161 us -> 161 us (level)
    all_to_all x1, waiting for transfers between devices: 20 us -> 22.1 us  [exchange(): return lax.all_to_all(x.reshape(n, -1, HD), 'chan', 0, 0).reshape(x.shape)]
  transfers between devices with their start and end apart: 7 -> 7, of which waited for: 4 -> 4; matrix products, arithmetic and copies ran while one was open for 1% -> 0% of each run, Pallas kernels for 0% -> 0%
where the time goes in v5:
time: 161 us; the launch traced here: 160 us
  blocking collectives  78.3 us (49%)
  starting transfers between devices  37.2 us (23%)
  waiting for transfers between devices  34.8 us (22%)
  Pallas kernels  7.34 us (5%)
  local copies, waits for them, and re-layouts  1.7 us (1%)
    all_to_all x2, blocking collectives, total_gram(): mine = jnp.sum(lax.all_to_all(parts, 'chan', 0, 0), axis=0, keepdims=True)  31.4 us
    all_to_all x2, blocking collectives, total_gram(): lax.all_to_all(jnp.broadcast_to(mine, parts.shape), 'chan', 0, 0)  29.6 us
    all_to_all x1, waiting for transfers between devices, exchange(): return lax.all_to_all(x.reshape(n, -1, HD), 'chan', 0, 0).reshape(x.shape)  22.1 us
    all_to_all x1, blocking collectives, exchange(): return lax.all_to_all(x.reshape(n, -1, HD), 'chan', 0, 0).reshape(x.shape)  17.3 us
    all_to_all x1, starting transfers between devices, exchange(): return lax.all_to_all(x.reshape(n, -1, HD), 'chan', 0, 0).reshape(x.shape)  14.5 us
    ppermute x3, starting transfers between devices, swap(): near = lax.ppermute(near, 'facet', beside + [(j, i) for i, j in beside])  12.9 us
    ppermute x3, waiting for transfers between devices, swap(): far = lax.ppermute(far, 'facet', apart + [(j, i) for i, j in apart])  12.7 us
    ppermute x3, starting transfers between devices, swap(): far = lax.ppermute(far, 'facet', apart + [(j, i) for i, j in apart])  9.76 us
  transfers between devices with their start and end apart: 7, of which 4 were waited for; matrix products, arithmetic and copies ran while one was open for 0% of the time, Pallas kernels for 0%

profile of v5, /device:TPU:17, one launch (start us, length us, event | category | flops | bytes accessed | tf_op | source)
XLA Modules:
  0.0 160.1 jit_solution(13352869966167665359)
XLA Ops:
  0.0 2.2 %shard_map.64 = f32[1536,128]{1,0:T(8,128)} custom-call(f32[512,128]{1,0:T(8,128)} %bitcast.28, f32[512,128]{1,0:T(8,128)} %bitcast.29, f32[512,128]{1,0:T(8,128)} %bitcast.30), custom_call_target="tpu_custom_call" | custom-call | tf_op jit(solution)/shard_map/pallas_call | solution.py:229
  2.2 14.5 %all-to-all-start = ((f32[64,24,128]{2,1,0:T(8,128)}), f32[64,24,128]{2,1,0:T(8,128)S(1)}, u32[]{:S(2)}, u32[]{:S(2)}) async-start(f32[64,24,128]{2,1,0:T(8,128)} %bitcast.3), calls=%async_computation | async-start | bytes 1572864 | tf_op jit(solution)/shard_map/all_to_all | solution.py:239
  16.8 22.1 %all-to-all-done = f32[64,24,128]{2,1,0:T(8,128)S(1)} async-done(((f32[64,24,128]{2,1,0:T(8,128)}), f32[64,24,128]{2,1,0:T(8,128)S(1)}, u32[]{:S(2)}, u32[]{:S(2)}) %all-to-all-start) | async-done | bytes 786464 | tf_op jit(solution)/shard_map/all_to_all | solution.py:239
  38.9 0.3 shard_map.65
  39.2 0.3 copy-done.1
  39.6 0.3 copy-done
  40.2 0.6 copy-done.2
  40.8 3.9 %collective-permute-start = (f32[128,128]{1,0:T(8,128)S(1)}, f32[128,128]{1,0:T(8,128)S(1)}, u32[]{:S(2)}, u32[]{:S(2)}) collective-permute-start(f32[128,128]{1,0:T(8,128)S(1)} %get-tuple-element.24), channel_id=1, source_target_pairs={{0,1},{2,3},{4,5},{6,7},{1,0},{3,2},{5,4},{7,6},{8,9},{10,11},{12,... | collective-permute-start | bytes 196616 | tf_op jit(solution)/shard_map/ppermute | solution.py:246
  44.8 4.4 %collective-permute-start.1 = (f32[128,128]{1,0:T(8,128)S(1)}, f32[128,128]{1,0:T(8,128)S(1)}, u32[]{:S(2)}, u32[]{:S(2)}) collective-permute-start(f32[128,128]{1,0:T(8,128)S(1)} %get-tuple-element.25), channel_id=1, source_target_pairs={{1,2},{3,4},{5,6},{2,1},{4,3},{6,5},{9,10},{11,12},{13,14},{10,9},... | collective-permute-start | bytes 196616 | tf_op jit(solution)/shard_map/ppermute | solution.py:247
  49.3 0.1 concatenate.3
  49.4 3.0 %collective-permute-done.1.far = f32[128,128]{1,0:T(8,128)S(1)} collective-permute-done((f32[128,128]{1,0:T(8,128)S(1)}, f32[128,128]{1,0:T(8,128)S(1)}, u32[]{:S(2)}, u32[]{:S(2)}) %collective-permute-start.1) | collective-permute-done | bytes 65568 | tf_op jit(solution)/shard_map/ppermute | solution.py:247
  52.5 0.6 shard_map.66
  53.0 17.3 %all_to_all.30 = f32[64,1,640]{2,1,0:T(1,128)S(1)} all-to-all(f32[64,1,640]{2,1,0:T(1,128)S(1)} %bitcast.27), channel_id=1, replica_groups=mesh['chan'=64,'facet'=8] {'chan'}, dimensions={0} | all-to-all | bytes 327680 | tf_op jit(solution)/shard_map/all_to_all | solution.py:253
  70.3 0.1 reduce_sum.18
  70.4 0.1 broadcast_in_dim.6
  70.5 14.0 %all_to_all.31 = f32[64,1,640]{2,1,0:T(1,128)S(1)} all-to-all(f32[64,1,640]{2,1,0:T(1,128)S(1)} %broadcast_in_dim.6), channel_id=1, replica_groups=mesh['chan'=64,'facet'=8] {'chan'}, dimensions={0} | all-to-all | bytes 327680 | tf_op jit(solution)/shard_map/all_to_all | solution.py:254
  84.5 1.4 shard_map.67
  85.9 4.5 %collective-permute-start.2 = (f32[128,128]{1,0:T(8,128)S(1)}, f32[128,128]{1,0:T(8,128)S(1)}, u32[]{:S(2)}, u32[]{:S(2)}) collective-permute-start(f32[128,128]{1,0:T(8,128)S(1)} %get-tuple-element.32), channel_id=1, source_target_pairs={{0,1},{2,3},{4,5},{6,7},{1,0},{3,2},{5,4},{7,6},{8,9},{10,11},{12,... | collective-permute-start | bytes 196616 | tf_op jit(solution)/shard_map/ppermute | solution.py:246
  90.4 3.1 %collective-permute-start.3 = (f32[128,128]{1,0:T(8,128)S(1)}, f32[128,128]{1,0:T(8,128)S(1)}, u32[]{:S(2)}, u32[]{:S(2)}) collective-permute-start(f32[128,128]{1,0:T(8,128)S(1)} %get-tuple-element.33), channel_id=1, source_target_pairs={{1,2},{3,4},{5,6},{2,1},{4,3},{6,5},{9,10},{11,12},{13,14},{10,9},... | collective-permute-start | bytes 196616 | tf_op jit(solution)/shard_map/ppermute | solution.py:247
  93.5 4.6 %collective-permute-done.3.s_far = f32[128,128]{1,0:T(8,128)S(1)} collective-permute-done((f32[128,128]{1,0:T(8,128)S(1)}, f32[128,128]{1,0:T(8,128)S(1)}, u32[]{:S(2)}, u32[]{:S(2)}) %collective-permute-start.3) | collective-permute-done | bytes 65568 | tf_op jit(solution)/shard_map/ppermute | solution.py:247
  98.1 0.7 shard_map.68
  98.8 14.1 %all_to_all.32 = f32[64,1,640]{2,1,0:T(1,128)S(1)} all-to-all(f32[64,1,640]{2,1,0:T(1,128)S(1)} %bitcast.26), channel_id=1, replica_groups=mesh['chan'=64,'facet'=8] {'chan'}, dimensions={0} | all-to-all | bytes 327680 | tf_op jit(solution)/shard_map/all_to_all | solution.py:253
  112.9 0.1 reduce_sum.19
  113.0 0.1 broadcast_in_dim.7
  113.1 15.6 %all_to_all.33 = f32[64,1,640]{2,1,0:T(1,128)S(1)} all-to-all(f32[64,1,640]{2,1,0:T(1,128)S(1)} %broadcast_in_dim.7), channel_id=1, replica_groups=mesh['chan'=64,'facet'=8] {'chan'}, dimensions={0} | all-to-all | bytes 327680 | tf_op jit(solution)/shard_map/all_to_all | solution.py:254
  128.7 1.3 shard_map.69
  130.0 4.5 %collective-permute-start.4 = (f32[64,128]{1,0:T(8,128)S(1)}, f32[64,128]{1,0:T(8,128)S(1)}, u32[]{:S(2)}, u32[]{:S(2)}) collective-permute-start(f32[64,128]{1,0:T(8,128)S(1)} %get-tuple-element.37), channel_id=1, source_target_pairs={{0,1},{2,3},{4,5},{6,7},{1,0},{3,2},{5,4},{7,6},{8,9},{10,11},{12,... | collective-permute-start | bytes 98312 | tf_op jit(solution)/shard_map/ppermute | solution.py:246
  134.4 2.2 %collective-permute-start.5 = (f32[64,128]{1,0:T(8,128)S(1)}, f32[64,128]{1,0:T(8,128)S(1)}, u32[]{:S(2)}, u32[]{:S(2)}) collective-permute-start(f32[64,128]{1,0:T(8,128)S(1)} %get-tuple-element.38), channel_id=1, source_target_pairs={{1,2},{3,4},{5,6},{2,1},{4,3},{6,5},{9,10},{11,12},{13,14},{10,9},... | collective-permute-start | bytes 98312 | tf_op jit(solution)/shard_map/ppermute | solution.py:247
  136.7 5.1 %collective-permute-done.5.far = f32[64,128]{1,0:T(8,128)S(1)} collective-permute-done((f32[64,128]{1,0:T(8,128)S(1)}, f32[64,128]{1,0:T(8,128)S(1)}, u32[]{:S(2)}, u32[]{:S(2)}) %collective-permute-start.5) | collective-permute-done | bytes 32800 | tf_op jit(solution)/shard_map/ppermute | solution.py:247
  141.8 0.2 shard_map.70
  142.0 17.3 %all_to_all.34 = f32[64,8,128]{2,1,0:T(8,128)S(1)} all-to-all(f32[64,8,128]{2,1,0:T(8,128)S(1)} %bitcast.23), channel_id=1, replica_groups=mesh['chan'=64,'facet'=8] {'chan'}, dimensions={0} | all-to-all | bytes 524288 | tf_op jit(solution)/shard_map/all_to_all | solution.py:239
  159.3 0.8 shard_map.71
  (20 shorter events, 0.5 us)
Async XLA Ops:
  2.2 36.7 %all-to-all-start = ((f32[64,24,128]{2,1,0:T(8,128)}), f32[64,24,128]{2,1,0:T(8,128)S(1)}, u32[]{:S(2)}, u32[]{:S(2)}) async-start(f32[64,24,128]{2,1,0:T(8,128)} %bitcast.3), calls=%async_computation | async-start | bytes 1572864 | tf_op jit(solution)/shard_map/all_to_all | solution.py:239
  38.9 0.7 copy-start.1
  39.2 0.7 copy-start
  40.1 0.7 copy-start.2
  40.8 8.6 %collective-permute-start = (f32[128,128]{1,0:T(8,128)S(1)}, f32[128,128]{1,0:T(8,128)S(1)}, u32[]{:S(2)}, u32[]{:S(2)}) collective-permute-start(f32[128,128]{1,0:T(8,128)S(1)} %get-tuple-element.24), channel_id=1, source_target_pairs={{0,1},{2,3},{4,5},{6,7},{1,0},{3,2},{5,4},{7,6},{8,9},{10,11},{12,... | collective-permute-start | bytes 196616 | tf_op jit(solution)/shard_map/ppermute | solution.py:246
  44.8 7.7 %collective-permute-start.1 = (f32[128,128]{1,0:T(8,128)S(1)}, f32[128,128]{1,0:T(8,128)S(1)}, u32[]{:S(2)}, u32[]{:S(2)}) collective-permute-start(f32[128,128]{1,0:T(8,128)S(1)} %get-tuple-element.25), channel_id=1, source_target_pairs={{1,2},{3,4},{5,6},{2,1},{4,3},{6,5},{9,10},{11,12},{13,14},{10,9},... | collective-permute-start | bytes 196616 | tf_op jit(solution)/shard_map/ppermute | solution.py:247
  85.9 7.7 %collective-permute-start.2 = (f32[128,128]{1,0:T(8,128)S(1)}, f32[128,128]{1,0:T(8,128)S(1)}, u32[]{:S(2)}, u32[]{:S(2)}) collective-permute-start(f32[128,128]{1,0:T(8,128)S(1)} %get-tuple-element.32), channel_id=1, source_target_pairs={{0,1},{2,3},{4,5},{6,7},{1,0},{3,2},{5,4},{7,6},{8,9},{10,11},{12,... | collective-permute-start | bytes 196616 | tf_op jit(solution)/shard_map/ppermute | solution.py:246
  90.4 7.7 %collective-permute-start.3 = (f32[128,128]{1,0:T(8,128)S(1)}, f32[128,128]{1,0:T(8,128)S(1)}, u32[]{:S(2)}, u32[]{:S(2)}) collective-permute-start(f32[128,128]{1,0:T(8,128)S(1)} %get-tuple-element.33), channel_id=1, source_target_pairs={{1,2},{3,4},{5,6},{2,1},{4,3},{6,5},{9,10},{11,12},{13,14},{10,9},... | collective-permute-start | bytes 196616 | tf_op jit(solution)/shard_map/ppermute | solution.py:247
  130.0 6.7 %collective-permute-start.4 = (f32[64,128]{1,0:T(8,128)S(1)}, f32[64,128]{1,0:T(8,128)S(1)}, u32[]{:S(2)}, u32[]{:S(2)}) collective-permute-start(f32[64,128]{1,0:T(8,128)S(1)} %get-tuple-element.37), channel_id=1, source_target_pairs={{0,1},{2,3},{4,5},{6,7},{1,0},{3,2},{5,4},{7,6},{8,9},{10,11},{12,... | collective-permute-start | bytes 98312 | tf_op jit(solution)/shard_map/ppermute | solution.py:246
  134.4 7.3 %collective-permute-start.5 = (f32[64,128]{1,0:T(8,128)S(1)}, f32[64,128]{1,0:T(8,128)S(1)}, u32[]{:S(2)}, u32[]{:S(2)}) collective-permute-start(f32[64,128]{1,0:T(8,128)S(1)} %get-tuple-element.38), channel_id=1, source_target_pairs={{1,2},{3,4},{5,6},{2,1},{4,3},{6,5},{9,10},{11,12},{13,14},{10,9},... | collective-permute-start | bytes 98312 | tf_op jit(solution)/shard_map/ppermute | solution.py:247

commit v6 on v5

--- a/solution.py
+++ b/solution.py
@@ -96,14 +96,27 @@
     return gram[...]
 
 
-def pack_body(est, dirty, weights, out):
+def pack_body(est, dirty, weights, margin, blend, tau, out, margin_out, blend_out, tau_out, buf, sems, small):
     n = out.shape[0] // (ARRAYS * G8)
-    for c in range(CL):
+    copies = []
+    for c in range(CL):
+        rows = pl.ds(c * WL * n, WL * n)
+        for a, ref in enumerate((est, dirty, weights)):
+            copies.append(pltpu.make_async_copy(ref.at[rows, :], buf.at[a, rows, :], sems.at[a, c]))
+            copies[-1].start()
+    for i, pair in enumerate(((margin, margin_out), (blend, blend_out), (tau, tau_out))):
+        copies.append(pltpu.make_async_copy(*pair, small.at[i]))
+        copies[-1].start()
+    for c in range(CL):
+        for a in range(ARRAYS):
+            copies[c * ARRAYS + a].wait()
         for w in range(WL):
             rows = pl.ds(c * WL * n + w, n, stride=WL)
-            e, d, k = est[rows, :], dirty[rows, :], weights[rows, :]
+            e, d, k = buf[0, rows, :], buf[1, rows, :], buf[2, rows, :]
             for a, value in enumerate((e - k * (e - d), d, k)):
                 out[pl.ds(a * G8 + c * WL + w, n, stride=ARRAYS * G8), :] = value
+    for copy in copies[CL * ARRAYS :]:
+        copy.wait()
 
 
 def is_even():
@@ -145,7 +158,7 @@
     put_gram(x, tri)
 
 
-def shrink_of(gram, x, factor):
+def kernel_of(gram, factor):
     count = gram.shape[0]
     row = lax.broadcasted_iota(jnp.int32, gram.shape, 0)
     identity = (row == lanes(gram.shape)).astype(F32)
@@ -158,20 +171,19 @@
     stepped = 1.5 * target - 0.5 * square
     twice = 2.25 * identity - 1.5 * target + 0.25 * square
     inverse_root = 1.5 * first - 0.5 * product(split(stepped), split(twice))
-    return product(split(identity - factor * inverse_root), split(x))
-
-
-def apply_body(step, tri, x, table, out, near, far, gram):
+    return identity - factor * inverse_root
+
+
+def put_rims(edges, n, near, far):
+    edges = [edges[pl.ds(c * n, n), :] for c in range(CL)]
+    near[0:n, :], far[0:n, :] = give(pack_edges(edges, 0), pack_edges(edges, WL * OV))
+
+
+def zone_body(tri, x, got, table, out, near, far, gram):
     n = x.shape[0] // CL
-    factor = table[3 + step : 4 + step, : gram.shape[0]]
-    out[...] = shrink_of(get_gram(tri, gram), x[...], factor) * table[1:2, :]
-    edges = [out[pl.ds(c * n, n), pl.ds(WL * HD, HD)] for c in range(CL)]
-    near[0:n, :], far[0:n, :] = give(pack_edges(edges, 0), pack_edges(edges, WL * OV))
-
-
-def zone_body(tri, x, got, table, out, near, far, gram):
-    apply_body(0, tri, x, table, out, near, far, gram)
-    n = x.shape[0] // CL
+    kernel = kernel_of(get_gram(tri, gram), table[3:4, : gram.shape[0]])
+    out[...] = product(split(kernel), split(x[...])) * table[1:2, :]
+    put_rims(out.at[:, pl.ds(WL * HD, HD)], n, near, far)
     pieces = []
     for g in range(G8):
         cols = pl.ds(g % WL * HD, HD)
@@ -203,6 +215,16 @@
     put_gram(x, tri)
 
 
+def last_body(tri, x, table, kernel, near, far, gram, edges):
+    kernel[...] = kernel_of(get_gram(tri, gram), table[4:5, : gram.shape[0]])
+    edges[...] = product(split(kernel[...]), split(x[:, WL * HD :])) * table[1:2, WL * HD :]
+    put_rims(edges, x.shape[0] // CL, near, far)
+
+
+def center_body(kernel, x, table, out):
+    out[...] = product(split(kernel[...]), split(x[:, : WL * HD])) * table[1:2, : WL * HD]
+
+
 def close_body(s, near, far, table, out):
     n = near.shape[0]
     center = take(near[...], far[...])
@@ -220,12 +242,11 @@
             out[pl.ds(c * WL * n + w, n, stride=WL), :] = got[pl.ds(c * WL + w, n, stride=G8), :]
 
 
-def run(body, shapes, *args, enter=True, leave=True, scratch=()):
+def run(body, shapes, *args, leave=True, scratch=()):
     spec = pl.BlockSpec(memory_space=pltpu.VMEM)
     outs = [pltpu.VMEM(s, F32) if leave else jax.ShapeDtypeStruct(s, F32) for s in shapes]
     single = len(outs) == 1
-    if enter:
-        args = [pltpu.with_memory_space_constraint(a, pltpu.VMEM) for a in args]
+    args = [pltpu.with_memory_space_constraint(a, pltpu.VMEM) for a in args]
     return pl.pallas_call(
         body,
         out_shape=outs[0] if single else outs,
@@ -282,31 +303,29 @@
     c, width = n * CL, (WL + 1) * HD
     assert estimate.shape == (CL, n * WL, HD)
     flat = (CL * WL * n, HD)
-    sent = run(
+    small = (margin.reshape(1, -1), blend_table, tau_steps.reshape(1, -1))
+    whole = pl.BlockSpec(memory_space=pltpu.VMEM)
+    sent, margin, blend_table, tau_steps = pl.pallas_call(
         pack_body,
-        [(ARRAYS * G8 * n, HD)],
-        estimate.reshape(flat),
-        dirty.reshape(flat),
-        weights.reshape(flat),
-        enter=False,
-    )
+        out_shape=[pltpu.VMEM((ARRAYS * G8 * n, HD), F32)] + [pltpu.VMEM(v.shape, jnp.int32) for v in small],
+        in_specs=[pl.BlockSpec(memory_space=pl.ANY)] * (ARRAYS + 3),
+        out_specs=[whole] * 4,
+        scratch_shapes=[pltpu.VMEM((ARRAYS,) + flat, F32), pltpu.SemaphoreType.DMA((ARRAYS, CL)), pltpu.SemaphoreType.DMA((3,))],
+        name="pack",
+    )(estimate.reshape(flat), dirty.reshape(flat), weights.reshape(flat), *small)
     got = exchange(sent, n)
     near, far = run(edge_body, [(2 * n, HD)] * 2, got)
-    near, far, *small = lax.optimization_barrier((near, far, margin, blend_table, tau_steps))
     near, far = swap(near, far)
-    table = tables(*small)
+    table = tables(margin[0], blend_table, tau_steps[0])
     sums = (n * pl.cdiv(c * (c + 1) // 2, n * HD), HD)
     x, gram = run(gram_body, [(c, width), sums], got, near, far, table)
     gram = total_gram(gram, n)
-    s, s_near, s_far = run(
-        zone_body, [(c, width), (2 * n, HD), (2 * n, HD)], gram, x, got, table, scratch=[(c, c)]
-    )
+    s, s_near, s_far = run(zone_body, [(c, width), (2 * n, HD), (2 * n, HD)], gram, x, got, table, scratch=[(c, c)])
     s_near, s_far = swap(s_near, s_far)
     x, gram = run(next_body, [(c, width), sums], got, near, far, s, s_near, s_far, table)
     gram = total_gram(gram, n)
-    s, s_near, s_far = run(
-        lambda *refs: apply_body(1, *refs), [(c, width), (n, HD), (n, HD)], gram, x, table, scratch=[(c, c)]
-    )
+    kernel, s_near, s_far = run(last_body, [(c, c), (n, HD), (n, HD)], gram, x, table, scratch=[(c, c), (c, HD)])
+    s = run(center_body, [(c, WL * HD)], kernel, x, table)
     s_near, s_far = swap(s_near, s_far)
     back = exchange(run(close_body, [(G8 * n, HD)], s, s_near, s_far, table), n)
     return run(unpack_body, [flat], back, leave=False).reshape(estimate.shape)

time: 161 us -> 159 us (0.988)
    pallas_call x0 -> x1, Pallas kernels: none -> 2.23 us  [per_device(): pl.pallas_call(pack_body, out_shape=[pltpu.VMEM((ARRAYS * G8 * n, HD), F3...]
    pallas_call x8, Pallas kernels: 7.34 us -> 5.3 us  [run(): pl.pallas_call(body, out_shape=outs[0] if single else outs, in_specs=[spe...]
where the time goes in v6:
time: 159 us; the launch traced here: 158 us
  blocking collectives  78.2 us (49%)
  starting transfers between devices  37.3 us (23%)
  waiting for transfers between devices  34.1 us (21%)
  Pallas kernels  7.53 us (5%)
    all_to_all x2, blocking collectives, total_gram(): mine = jnp.sum(lax.all_to_all(parts, 'chan', 0, 0), axis=0, keepdims=True)  31.4 us
    all_to_all x2, blocking collectives, total_gram(): lax.all_to_all(jnp.broadcast_to(mine, parts.shape), 'chan', 0, 0)  29.6 us
    all_to_all x1, waiting for transfers between devices, exchange(): return lax.all_to_all(x.reshape(n, -1, HD), 'chan', 0, 0).reshape(x.shape)  21.6 us
    all_to_all x1, blocking collectives, exchange(): return lax.all_to_all(x.reshape(n, -1, HD), 'chan', 0, 0).reshape(x.shape)  17.3 us
    all_to_all x1, starting transfers between devices, exchange(): return lax.all_to_all(x.reshape(n, -1, HD), 'chan', 0, 0).reshape(x.shape)  14.5 us
    ppermute x3, starting transfers between devices, swap(): near = lax.ppermute(near, 'facet', beside + [(j, i) for i, j in beside])  13 us
    ppermute x3, waiting for transfers between devices, swap(): far = lax.ppermute(far, 'facet', apart + [(j, i) for i, j in apart])  12.6 us
    ppermute x3, starting transfers between devices, swap(): far = lax.ppermute(far, 'facet', apart + [(j, i) for i, j in apart])  9.77 us
  transfers between devices with their start and end apart: 7, of which 4 were waited for; matrix products, arithmetic and copies ran while one was open for 0% of the time, Pallas kernels for 0%

profile of v6, /device:TPU:17, one launch (start us, length us, event | category | flops | bytes accessed | tf_op | source)
XLA Modules:
  0.0 158.4 jit_solution(978830627944248299)
XLA Ops:
  0.0 2.2 %pack.1 = (f32[1536,128]{1,0:T(8,128)}, s32[1,8]{1,0:T(1,128)S(1)}, s32[8,160]{1,0:T(8,128)S(1)}, s32[1,2]{1,0:T(1,128)S(1)}) custom-call(f32[512,128]{1,0:T(8,128)} %bitcast.36, f32[512,128]{1,0:T(8,128)} %bitcast.37, f32[512,128]{1,0:T(8,128)} %bitcast.38, s32[1,8]{1,0:T(1,128)} %bitcast.41, s32[8,160]{1,0:T(8,128)} %blend.1, s32[1,2]{1,0:T(1,128)} %bitcast.42), custom_call_target="tpu_custom_call" | custom-call | tf_op jit(solution)/shard_map/pack/pallas_call | solution.py:308
  2.2 14.5 %all-to-all-start = ((f32[64,24,128]{2,1,0:T(8,128)}), f32[64,24,128]{2,1,0:T(8,128)S(1)}, u32[]{:S(2)}, u32[]{:S(2)}) async-start(f32[64,24,128]{2,1,0:T(8,128)} %bitcast.5), calls=%async_computation | async-start | bytes 1572864 | tf_op jit(solution)/shard_map/all_to_all | solution.py:260
  16.9 0.1 fusion
  17.1 0.1 pad.19
  17.3 0.1 concatenate.3
  17.4 21.6 %all-to-all-done = f32[64,24,128]{2,1,0:T(8,128)S(1)} async-done(((f32[64,24,128]{2,1,0:T(8,128)}), f32[64,24,128]{2,1,0:T(8,128)S(1)}, u32[]{:S(2)}, u32[]{:S(2)}) %all-to-all-start) | async-done | bytes 786464 | tf_op jit(solution)/shard_map/all_to_all | solution.py:260
  38.9 0.3 shard_map.64
  39.2 4.0 %collective-permute-start = (f32[128,128]{1,0:T(8,128)S(1)}, f32[128,128]{1,0:T(8,128)S(1)}, u32[]{:S(2)}, u32[]{:S(2)}) collective-permute-start(f32[128,128]{1,0:T(8,128)S(1)} %get-tuple-element.22), channel_id=1, source_target_pairs={{0,1},{2,3},{4,5},{6,7},{1,0},{3,2},{5,4},{7,6},{8,9},{10,11},{12,... | collective-permute-start | bytes 196616 | tf_op jit(solution)/shard_map/ppermute | solution.py:267
  43.2 4.4 %collective-permute-start.1 = (f32[128,128]{1,0:T(8,128)S(1)}, f32[128,128]{1,0:T(8,128)S(1)}, u32[]{:S(2)}, u32[]{:S(2)}) collective-permute-start(f32[128,128]{1,0:T(8,128)S(1)} %get-tuple-element.23), channel_id=1, source_target_pairs={{1,2},{3,4},{5,6},{2,1},{4,3},{6,5},{9,10},{11,12},{13,14},{10,9},... | collective-permute-start | bytes 196616 | tf_op jit(solution)/shard_map/ppermute | solution.py:268
  47.7 3.2 %collective-permute-done.1.far = f32[128,128]{1,0:T(8,128)S(1)} collective-permute-done((f32[128,128]{1,0:T(8,128)S(1)}, f32[128,128]{1,0:T(8,128)S(1)}, u32[]{:S(2)}, u32[]{:S(2)}) %collective-permute-start.1) | collective-permute-done | bytes 65568 | tf_op jit(solution)/shard_map/ppermute | solution.py:268
  50.9 0.6 shard_map.65
  51.5 17.2 %all_to_all.30 = f32[64,1,640]{2,1,0:T(1,128)S(1)} all-to-all(f32[64,1,640]{2,1,0:T(1,128)S(1)} %bitcast.35), channel_id=1, replica_groups=mesh['chan'=64,'facet'=8] {'chan'}, dimensions={0} | all-to-all | bytes 327680 | tf_op jit(solution)/shard_map/all_to_all | solution.py:274
  68.7 0.1 reduce_sum.18
  68.9 0.1 broadcast_in_dim.6
  68.9 14.0 %all_to_all.31 = f32[64,1,640]{2,1,0:T(1,128)S(1)} all-to-all(f32[64,1,640]{2,1,0:T(1,128)S(1)} %broadcast_in_dim.6), channel_id=1, replica_groups=mesh['chan'=64,'facet'=8] {'chan'}, dimensions={0} | all-to-all | bytes 327680 | tf_op jit(solution)/shard_map/all_to_all | solution.py:275
  83.0 1.4 shard_map.66
  84.3 4.5 %collective-permute-start.2 = (f32[128,128]{1,0:T(8,128)S(1)}, f32[128,128]{1,0:T(8,128)S(1)}, u32[]{:S(2)}, u32[]{:S(2)}) collective-permute-start(f32[128,128]{1,0:T(8,128)S(1)} %get-tuple-element.30), channel_id=1, source_target_pairs={{0,1},{2,3},{4,5},{6,7},{1,0},{3,2},{5,4},{7,6},{8,9},{10,11},{12,... | collective-permute-start | bytes 196616 | tf_op jit(solution)/shard_map/ppermute | solution.py:267
  88.8 3.1 %collective-permute-start.3 = (f32[128,128]{1,0:T(8,128)S(1)}, f32[128,128]{1,0:T(8,128)S(1)}, u32[]{:S(2)}, u32[]{:S(2)}) collective-permute-start(f32[128,128]{1,0:T(8,128)S(1)} %get-tuple-element.31), channel_id=1, source_target_pairs={{1,2},{3,4},{5,6},{2,1},{4,3},{6,5},{9,10},{11,12},{13,14},{10,9},... | collective-permute-start | bytes 196616 | tf_op jit(solution)/shard_map/ppermute | solution.py:268
  92.0 4.6 %collective-permute-done.3.s_far = f32[128,128]{1,0:T(8,128)S(1)} collective-permute-done((f32[128,128]{1,0:T(8,128)S(1)}, f32[128,128]{1,0:T(8,128)S(1)}, u32[]{:S(2)}, u32[]{:S(2)}) %collective-permute-start.3) | collective-permute-done | bytes 65568 | tf_op jit(solution)/shard_map/ppermute | solution.py:268
  96.5 0.7 shard_map.67
  97.2 14.1 %all_to_all.32 = f32[64,1,640]{2,1,0:T(1,128)S(1)} all-to-all(f32[64,1,640]{2,1,0:T(1,128)S(1)} %bitcast.34), channel_id=1, replica_groups=mesh['chan'=64,'facet'=8] {'chan'}, dimensions={0} | all-to-all | bytes 327680 | tf_op jit(solution)/shard_map/all_to_all | solution.py:274
  111.3 0.1 reduce_sum.19
  111.4 0.1 broadcast_in_dim.7
  111.5 15.6 %all_to_all.33 = f32[64,1,640]{2,1,0:T(1,128)S(1)} all-to-all(f32[64,1,640]{2,1,0:T(1,128)S(1)} %broadcast_in_dim.7), channel_id=1, replica_groups=mesh['chan'=64,'facet'=8] {'chan'}, dimensions={0} | all-to-all | bytes 327680 | tf_op jit(solution)/shard_map/all_to_all | solution.py:275
  127.1 1.2 shard_map.68
  128.3 4.5 %collective-permute-start.4 = (f32[64,128]{1,0:T(8,128)S(1)}, f32[64,128]{1,0:T(8,128)S(1)}, u32[]{:S(2)}, u32[]{:S(2)}) collective-permute-start(f32[64,128]{1,0:T(8,128)S(1)} %get-tuple-element.35), channel_id=1, source_target_pairs={{0,1},{2,3},{4,5},{6,7},{1,0},{3,2},{5,4},{7,6},{8,9},{10,11},{12,... | collective-permute-start | bytes 98312 | tf_op jit(solution)/shard_map/ppermute | solution.py:267
  132.8 2.2 %collective-permute-start.5 = (f32[64,128]{1,0:T(8,128)S(1)}, f32[64,128]{1,0:T(8,128)S(1)}, u32[]{:S(2)}, u32[]{:S(2)}) collective-permute-start(f32[64,128]{1,0:T(8,128)S(1)} %get-tuple-element.36), channel_id=1, source_target_pairs={{1,2},{3,4},{5,6},{2,1},{4,3},{6,5},{9,10},{11,12},{13,14},{10,9},... | collective-permute-start | bytes 98312 | tf_op jit(solution)/shard_map/ppermute | solution.py:268
  135.0 0.3 shard_map.69.s
  135.3 4.8 %collective-permute-done.5.far = f32[64,128]{1,0:T(8,128)S(1)} collective-permute-done((f32[64,128]{1,0:T(8,128)S(1)}, f32[64,128]{1,0:T(8,128)S(1)}, u32[]{:S(2)}, u32[]{:S(2)}) %collective-permute-start.5) | collective-permute-done | bytes 32800 | tf_op jit(solution)/shard_map/ppermute | solution.py:268
  140.1 0.2 shard_map.70
  140.3 17.3 %all_to_all.34 = f32[64,8,128]{2,1,0:T(8,128)S(1)} all-to-all(f32[64,8,128]{2,1,0:T(8,128)S(1)} %bitcast.30), channel_id=1, replica_groups=mesh['chan'=64,'facet'=8] {'chan'}, dimensions={0} | all-to-all | bytes 524288 | tf_op jit(solution)/shard_map/all_to_all | solution.py:260
  157.6 0.8 shard_map.71
  (15 shorter events, 0.4 us)
Async XLA Ops:
  2.2 36.7 %all-to-all-start = ((f32[64,24,128]{2,1,0:T(8,128)}), f32[64,24,128]{2,1,0:T(8,128)S(1)}, u32[]{:S(2)}, u32[]{:S(2)}) async-start(f32[64,24,128]{2,1,0:T(8,128)} %bitcast.5), calls=%async_computation | async-start | bytes 1572864 | tf_op jit(solution)/shard_map/all_to_all | solution.py:260
  39.2 8.5 %collective-permute-start = (f32[128,128]{1,0:T(8,128)S(1)}, f32[128,128]{1,0:T(8,128)S(1)}, u32[]{:S(2)}, u32[]{:S(2)}) collective-permute-start(f32[128,128]{1,0:T(8,128)S(1)} %get-tuple-element.22), channel_id=1, source_target_pairs={{0,1},{2,3},{4,5},{6,7},{1,0},{3,2},{5,4},{7,6},{8,9},{10,11},{12,... | collective-permute-start | bytes 196616 | tf_op jit(solution)/shard_map/ppermute | solution.py:267
  43.2 7.7 %collective-permute-start.1 = (f32[128,128]{1,0:T(8,128)S(1)}, f32[128,128]{1,0:T(8,128)S(1)}, u32[]{:S(2)}, u32[]{:S(2)}) collective-permute-start(f32[128,128]{1,0:T(8,128)S(1)} %get-tuple-element.23), channel_id=1, source_target_pairs={{1,2},{3,4},{5,6},{2,1},{4,3},{6,5},{9,10},{11,12},{13,14},{10,9},... | collective-permute-start | bytes 196616 | tf_op jit(solution)/shard_map/ppermute | solution.py:268
  84.3 7.7 %collective-permute-start.2 = (f32[128,128]{1,0:T(8,128)S(1)}, f32[128,128]{1,0:T(8,128)S(1)}, u32[]{:S(2)}, u32[]{:S(2)}) collective-permute-start(f32[128,128]{1,0:T(8,128)S(1)} %get-tuple-element.30), channel_id=1, source_target_pairs={{0,1},{2,3},{4,5},{6,7},{1,0},{3,2},{5,4},{7,6},{8,9},{10,11},{12,... | collective-permute-start | bytes 196616 | tf_op jit(solution)/shard_map/ppermute | solution.py:267
  88.8 7.7 %collective-permute-start.3 = (f32[128,128]{1,0:T(8,128)S(1)}, f32[128,128]{1,0:T(8,128)S(1)}, u32[]{:S(2)}, u32[]{:S(2)}) collective-permute-start(f32[128,128]{1,0:T(8,128)S(1)} %get-tuple-element.31), channel_id=1, source_target_pairs={{1,2},{3,4},{5,6},{2,1},{4,3},{6,5},{9,10},{11,12},{13,14},{10,9},... | collective-permute-start | bytes 196616 | tf_op jit(solution)/shard_map/ppermute | solution.py:268
  128.3 7.0 %collective-permute-start.4 = (f32[64,128]{1,0:T(8,128)S(1)}, f32[64,128]{1,0:T(8,128)S(1)}, u32[]{:S(2)}, u32[]{:S(2)}) collective-permute-start(f32[64,128]{1,0:T(8,128)S(1)} %get-tuple-element.35), channel_id=1, source_target_pairs={{0,1},{2,3},{4,5},{6,7},{1,0},{3,2},{5,4},{7,6},{8,9},{10,11},{12,... | collective-permute-start | bytes 98312 | tf_op jit(solution)/shard_map/ppermute | solution.py:267
  132.8 7.3 %collective-permute-start.5 = (f32[64,128]{1,0:T(8,128)S(1)}, f32[64,128]{1,0:T(8,128)S(1)}, u32[]{:S(2)}, u32[]{:S(2)}) collective-permute-start(f32[64,128]{1,0:T(8,128)S(1)} %get-tuple-element.36), channel_id=1, source_target_pairs={{1,2},{3,4},{5,6},{2,1},{4,3},{6,5},{9,10},{11,12},{13,14},{10,9},... | collective-permute-start | bytes 98312 | tf_op jit(solution)/shard_map/ppermute | solution.py:268

commit v7 on v6

--- a/solution.py
+++ b/solution.py
@@ -146,16 +146,22 @@
         near[rows, :], far[rows, :] = give(pack_center(pieces, 0), pack_center(pieces, HD - OV))
 
 
-def gram_body(got, near, far, table, x, tri):
+def inner_body(got, x, tri):
+    n = got.shape[0] // (ARRAYS * G8)
+    for c in range(CL):
+        for w in range(WL):
+            x[pl.ds(c * n, n), pl.ds(w * HD, HD)] = piece(got, 0, c * WL + w)
+    put_gram(x, tri)
+
+
+def gram_body(inner, near, far, table, edges, tri):
     n = near.shape[0] // 2
     keep = table[0:1, WL * HD :]
     before, after = take(near[0:n, :], far[0:n, :])
     for c in range(CL):
-        rows = pl.ds(c * n, n)
-        for w in range(WL):
-            x[rows, pl.ds(w * HD, HD)] = piece(got, 0, c * WL + w)
-        x[rows, pl.ds(WL * HD, HD)] = open_edges(before, after, c) * keep
-    put_gram(x, tri)
+        edges[pl.ds(c * n, n), :] = open_edges(before, after, c) * keep
+    put_gram(edges, tri)
+    tri[...] += inner[...]
 
 
 def kernel_of(gram, factor):
@@ -179,10 +185,11 @@
     near[0:n, :], far[0:n, :] = give(pack_edges(edges, 0), pack_edges(edges, WL * OV))
 
 
-def zone_body(tri, x, got, table, out, near, far, gram):
+def zone_body(tri, x, rims, got, table, out, near, far, gram):
     n = x.shape[0] // CL
-    kernel = kernel_of(get_gram(tri, gram), table[3:4, : gram.shape[0]])
-    out[...] = product(split(kernel), split(x[...])) * table[1:2, :]
+    kernel = split(kernel_of(get_gram(tri, gram), table[3:4, : gram.shape[0]]))
+    for cols, part in ((slice(0, WL * HD), x), (slice(WL * HD, WL * HD + HD), rims)):
+        out[:, cols] = product(kernel, split(part[...])) * table[1:2, cols]
     put_rims(out.at[:, pl.ds(WL * HD, HD)], n, near, far)
     pieces = []
     for g in range(G8):
@@ -318,9 +325,12 @@
     near, far = swap(near, far)
     table = tables(margin[0], blend_table, tau_steps[0])
     sums = (n * pl.cdiv(c * (c + 1) // 2, n * HD), HD)
-    x, gram = run(gram_body, [(c, width), sums], got, near, far, table)
+    x, inner = run(inner_body, [(c, WL * HD), sums], got)
+    rims, gram = run(gram_body, [(c, HD), sums], inner, near, far, table)
     gram = total_gram(gram, n)
-    s, s_near, s_far = run(zone_body, [(c, width), (2 * n, HD), (2 * n, HD)], gram, x, got, table, scratch=[(c, c)])
+    s, s_near, s_far = run(
+        zone_body, [(c, width), (2 * n, HD), (2 * n, HD)], gram, x, rims, got, table, scratch=[(c, c)]
+    )
     s_near, s_far = swap(s_near, s_far)
     x, gram = run(next_body, [(c, width), sums], got, near, far, s, s_near, s_far, table)
     gram = total_gram(gram, n)

time: 159 us -> 159 us (level)
    pallas_call x8 -> x9, Pallas kernels: 5.3 us -> 5.47 us  [run(): pl.pallas_call(body, out_shape=outs[0] if single else outs, in_specs=[spe...]
where the time goes in v7:
time: 159 us; the launch traced here: 158 us
  blocking collectives  78.3 us (49%)
  starting transfers between devices  37.2 us (23%)
  waiting for transfers between devices  33.8 us (21%)
  Pallas kernels  7.72 us (5%)
    all_to_all x2, blocking collectives, total_gram(): mine = jnp.sum(lax.all_to_all(parts, 'chan', 0, 0), axis=0, keepdims=True)  31.4 us
    all_to_all x2, blocking collectives, total_gram(): lax.all_to_all(jnp.broadcast_to(mine, parts.shape), 'chan', 0, 0)  29.6 us
    all_to_all x1, waiting for transfers between devices, exchange(): return lax.all_to_all(x.reshape(n, -1, HD), 'chan', 0, 0).reshape(x.shape)  21.6 us
    all_to_all x1, blocking collectives, exchange(): return lax.all_to_all(x.reshape(n, -1, HD), 'chan', 0, 0).reshape(x.shape)  17.3 us
    all_to_all x1, starting transfers between devices, exchange(): return lax.all_to_all(x.reshape(n, -1, HD), 'chan', 0, 0).reshape(x.shape)  14.5 us
    ppermute x3, starting transfers between devices, swap(): near = lax.ppermute(near, 'facet', beside + [(j, i) for i, j in beside])  13 us
    ppermute x3, waiting for transfers between devices, swap(): far = lax.ppermute(far, 'facet', apart + [(j, i) for i, j in apart])  12.2 us
    ppermute x3, starting transfers between devices, swap(): far = lax.ppermute(far, 'facet', apart + [(j, i) for i, j in apart])  9.76 us
  transfers between devices with their start and end apart: 7, of which 4 were waited for; matrix products, arithmetic and copies ran while one was open for 0% of the time, Pallas kernels for 0%

profile of v7, /device:TPU:17, one launch (start us, length us, event | category | flops | bytes accessed | tf_op | source)
XLA Modules:
  0.0 158.3 jit_solution(2752383503503652781)
XLA Ops:
  0.0 2.2 %pack.1 = (f32[1536,128]{1,0:T(8,128)}, s32[1,8]{1,0:T(1,128)S(1)}, s32[8,160]{1,0:T(8,128)S(1)}, s32[1,2]{1,0:T(1,128)S(1)}) custom-call(f32[512,128]{1,0:T(8,128)} %bitcast.36, f32[512,128]{1,0:T(8,128)} %bitcast.37, f32[512,128]{1,0:T(8,128)} %bitcast.38, s32[1,8]{1,0:T(1,128)} %bitcast.41, s32[8,160]{1,0:T(8,128)} %blend.1, s32[1,2]{1,0:T(1,128)} %bitcast.42), custom_call_target="tpu_custom_call" | custom-call | tf_op jit(solution)/shard_map/pack/pallas_call | solution.py:315
  2.3 14.5 %all-to-all-start = ((f32[64,24,128]{2,1,0:T(8,128)}), f32[64,24,128]{2,1,0:T(8,128)S(1)}, u32[]{:S(2)}, u32[]{:S(2)}) async-start(f32[64,24,128]{2,1,0:T(8,128)} %bitcast.5), calls=%async_computation | async-start | bytes 1572864 | tf_op jit(solution)/shard_map/all_to_all | solution.py:267
  17.1 0.1 pad.19
  17.3 0.1 concatenate.3
  17.4 21.6 %all-to-all-done = f32[64,24,128]{2,1,0:T(8,128)S(1)} async-done(((f32[64,24,128]{2,1,0:T(8,128)}), f32[64,24,128]{2,1,0:T(8,128)S(1)}, u32[]{:S(2)}, u32[]{:S(2)}) %all-to-all-start) | async-done | bytes 786464 | tf_op jit(solution)/shard_map/all_to_all | solution.py:267
  38.9 0.3 shard_map.64
  39.3 4.0 %collective-permute-start = (f32[128,128]{1,0:T(8,128)S(1)}, f32[128,128]{1,0:T(8,128)S(1)}, u32[]{:S(2)}, u32[]{:S(2)}) collective-permute-start(f32[128,128]{1,0:T(8,128)S(1)} %get-tuple-element.24), channel_id=1, source_target_pairs={{0,1},{2,3},{4,5},{6,7},{1,0},{3,2},{5,4},{7,6},{8,9},{10,11},{12,... | collective-permute-start | bytes 196616 | tf_op jit(solution)/shard_map/ppermute | solution.py:274
  43.2 4.4 %collective-permute-start.1 = (f32[128,128]{1,0:T(8,128)S(1)}, f32[128,128]{1,0:T(8,128)S(1)}, u32[]{:S(2)}, u32[]{:S(2)}) collective-permute-start(f32[128,128]{1,0:T(8,128)S(1)} %get-tuple-element.25), channel_id=1, source_target_pairs={{1,2},{3,4},{5,6},{2,1},{4,3},{6,5},{9,10},{11,12},{13,14},{10,9},... | collective-permute-start | bytes 196616 | tf_op jit(solution)/shard_map/ppermute | solution.py:275
  47.7 0.3 shard_map.65
  48.1 2.9 %collective-permute-done.1.far = f32[128,128]{1,0:T(8,128)S(1)} collective-permute-done((f32[128,128]{1,0:T(8,128)S(1)}, f32[128,128]{1,0:T(8,128)S(1)}, u32[]{:S(2)}, u32[]{:S(2)}) %collective-permute-start.1) | collective-permute-done | bytes 65568 | tf_op jit(solution)/shard_map/ppermute | solution.py:275
  50.9 0.4 shard_map.66
  51.3 17.3 %all_to_all.30 = f32[64,1,640]{2,1,0:T(1,128)S(1)} all-to-all(f32[64,1,640]{2,1,0:T(1,128)S(1)} %bitcast.35), channel_id=1, replica_groups=mesh['chan'=64,'facet'=8] {'chan'}, dimensions={0} | all-to-all | bytes 327680 | tf_op jit(solution)/shard_map/all_to_all | solution.py:281
  68.6 0.1 reduce_sum.18
  68.7 0.1 broadcast_in_dim.6
  68.8 14.0 %all_to_all.31 = f32[64,1,640]{2,1,0:T(1,128)S(1)} all-to-all(f32[64,1,640]{2,1,0:T(1,128)S(1)} %broadcast_in_dim.6), channel_id=1, replica_groups=mesh['chan'=64,'facet'=8] {'chan'}, dimensions={0} | all-to-all | bytes 327680 | tf_op jit(solution)/shard_map/all_to_all | solution.py:282
  82.8 1.4 shard_map.67
  84.2 4.5 %collective-permute-start.2 = (f32[128,128]{1,0:T(8,128)S(1)}, f32[128,128]{1,0:T(8,128)S(1)}, u32[]{:S(2)}, u32[]{:S(2)}) collective-permute-start(f32[128,128]{1,0:T(8,128)S(1)} %get-tuple-element.34), channel_id=1, source_target_pairs={{0,1},{2,3},{4,5},{6,7},{1,0},{3,2},{5,4},{7,6},{8,9},{10,11},{12,... | collective-permute-start | bytes 196616 | tf_op jit(solution)/shard_map/ppermute | solution.py:274
  88.7 3.1 %collective-permute-start.3 = (f32[128,128]{1,0:T(8,128)S(1)}, f32[128,128]{1,0:T(8,128)S(1)}, u32[]{:S(2)}, u32[]{:S(2)}) collective-permute-start(f32[128,128]{1,0:T(8,128)S(1)} %get-tuple-element.35), channel_id=1, source_target_pairs={{1,2},{3,4},{5,6},{2,1},{4,3},{6,5},{9,10},{11,12},{13,14},{10,9},... | collective-permute-start | bytes 196616 | tf_op jit(solution)/shard_map/ppermute | solution.py:275
  91.9 4.6 %collective-permute-done.3.s_far = f32[128,128]{1,0:T(8,128)S(1)} collective-permute-done((f32[128,128]{1,0:T(8,128)S(1)}, f32[128,128]{1,0:T(8,128)S(1)}, u32[]{:S(2)}, u32[]{:S(2)}) %collective-permute-start.3) | collective-permute-done | bytes 65568 | tf_op jit(solution)/shard_map/ppermute | solution.py:275
  96.4 0.7 shard_map.68
  97.1 14.1 %all_to_all.32 = f32[64,1,640]{2,1,0:T(1,128)S(1)} all-to-all(f32[64,1,640]{2,1,0:T(1,128)S(1)} %bitcast.34), channel_id=1, replica_groups=mesh['chan'=64,'facet'=8] {'chan'}, dimensions={0} | all-to-all | bytes 327680 | tf_op jit(solution)/shard_map/all_to_all | solution.py:281
  111.2 0.1 reduce_sum.19
  111.3 0.1 broadcast_in_dim.7
  111.4 15.6 %all_to_all.33 = f32[64,1,640]{2,1,0:T(1,128)S(1)} all-to-all(f32[64,1,640]{2,1,0:T(1,128)S(1)} %broadcast_in_dim.7), channel_id=1, replica_groups=mesh['chan'=64,'facet'=8] {'chan'}, dimensions={0} | all-to-all | bytes 327680 | tf_op jit(solution)/shard_map/all_to_all | solution.py:282
  127.0 1.2 shard_map.69
  128.2 4.5 %collective-permute-start.4 = (f32[64,128]{1,0:T(8,128)S(1)}, f32[64,128]{1,0:T(8,128)S(1)}, u32[]{:S(2)}, u32[]{:S(2)}) collective-permute-start(f32[64,128]{1,0:T(8,128)S(1)} %get-tuple-element.39), channel_id=1, source_target_pairs={{0,1},{2,3},{4,5},{6,7},{1,0},{3,2},{5,4},{7,6},{8,9},{10,11},{12,... | collective-permute-start | bytes 98312 | tf_op jit(solution)/shard_map/ppermute | solution.py:274
  132.7 2.2 %collective-permute-start.5 = (f32[64,128]{1,0:T(8,128)S(1)}, f32[64,128]{1,0:T(8,128)S(1)}, u32[]{:S(2)}, u32[]{:S(2)}) collective-permute-start(f32[64,128]{1,0:T(8,128)S(1)} %get-tuple-element.40), channel_id=1, source_target_pairs={{1,2},{3,4},{5,6},{2,1},{4,3},{6,5},{9,10},{11,12},{13,14},{10,9},... | collective-permute-start | bytes 98312 | tf_op jit(solution)/shard_map/ppermute | solution.py:275
  134.9 0.3 shard_map.70.s
  135.2 4.8 %collective-permute-done.5.far = f32[64,128]{1,0:T(8,128)S(1)} collective-permute-done((f32[64,128]{1,0:T(8,128)S(1)}, f32[64,128]{1,0:T(8,128)S(1)}, u32[]{:S(2)}, u32[]{:S(2)}) %collective-permute-start.5) | collective-permute-done | bytes 32800 | tf_op jit(solution)/shard_map/ppermute | solution.py:275
  140.0 0.2 shard_map.71
  140.2 17.3 %all_to_all.34 = f32[64,8,128]{2,1,0:T(8,128)S(1)} all-to-all(f32[64,8,128]{2,1,0:T(8,128)S(1)} %bitcast.30), channel_id=1, replica_groups=mesh['chan'=64,'facet'=8] {'chan'}, dimensions={0} | all-to-all | bytes 524288 | tf_op jit(solution)/shard_map/all_to_all | solution.py:267
  157.5 0.8 shard_map.72
  (16 shorter events, 0.4 us)
Async XLA Ops:
  2.3 36.7 %all-to-all-start = ((f32[64,24,128]{2,1,0:T(8,128)}), f32[64,24,128]{2,1,0:T(8,128)S(1)}, u32[]{:S(2)}, u32[]{:S(2)}) async-start(f32[64,24,128]{2,1,0:T(8,128)} %bitcast.5), calls=%async_computation | async-start | bytes 1572864 | tf_op jit(solution)/shard_map/all_to_all | solution.py:267
  39.3 8.8 %collective-permute-start = (f32[128,128]{1,0:T(8,128)S(1)}, f32[128,128]{1,0:T(8,128)S(1)}, u32[]{:S(2)}, u32[]{:S(2)}) collective-permute-start(f32[128,128]{1,0:T(8,128)S(1)} %get-tuple-element.24), channel_id=1, source_target_pairs={{0,1},{2,3},{4,5},{6,7},{1,0},{3,2},{5,4},{7,6},{8,9},{10,11},{12,... | collective-permute-start | bytes 196616 | tf_op jit(solution)/shard_map/ppermute | solution.py:274
  43.2 7.7 %collective-permute-start.1 = (f32[128,128]{1,0:T(8,128)S(1)}, f32[128,128]{1,0:T(8,128)S(1)}, u32[]{:S(2)}, u32[]{:S(2)}) collective-permute-start(f32[128,128]{1,0:T(8,128)S(1)} %get-tuple-element.25), channel_id=1, source_target_pairs={{1,2},{3,4},{5,6},{2,1},{4,3},{6,5},{9,10},{11,12},{13,14},{10,9},... | collective-permute-start | bytes 196616 | tf_op jit(solution)/shard_map/ppermute | solution.py:275
  84.2 7.7 %collective-permute-start.2 = (f32[128,128]{1,0:T(8,128)S(1)}, f32[128,128]{1,0:T(8,128)S(1)}, u32[]{:S(2)}, u32[]{:S(2)}) collective-permute-start(f32[128,128]{1,0:T(8,128)S(1)} %get-tuple-element.34), channel_id=1, source_target_pairs={{0,1},{2,3},{4,5},{6,7},{1,0},{3,2},{5,4},{7,6},{8,9},{10,11},{12,... | collective-permute-start | bytes 196616 | tf_op jit(solution)/shard_map/ppermute | solution.py:274
  88.7 7.7 %collective-permute-start.3 = (f32[128,128]{1,0:T(8,128)S(1)}, f32[128,128]{1,0:T(8,128)S(1)}, u32[]{:S(2)}, u32[]{:S(2)}) collective-permute-start(f32[128,128]{1,0:T(8,128)S(1)} %get-tuple-element.35), channel_id=1, source_target_pairs={{1,2},{3,4},{5,6},{2,1},{4,3},{6,5},{9,10},{11,12},{13,14},{10,9},... | collective-permute-start | bytes 196616 | tf_op jit(solution)/shard_map/ppermute | solution.py:275
  128.2 7.0 %collective-permute-start.4 = (f32[64,128]{1,0:T(8,128)S(1)}, f32[64,128]{1,0:T(8,128)S(1)}, u32[]{:S(2)}, u32[]{:S(2)}) collective-permute-start(f32[64,128]{1,0:T(8,128)S(1)} %get-tuple-element.39), channel_id=1, source_target_pairs={{0,1},{2,3},{4,5},{6,7},{1,0},{3,2},{5,4},{7,6},{8,9},{10,11},{12,... | collective-permute-start | bytes 98312 | tf_op jit(solution)/shard_map/ppermute | solution.py:274
  132.7 7.3 %collective-permute-start.5 = (f32[64,128]{1,0:T(8,128)S(1)}, f32[64,128]{1,0:T(8,128)S(1)}, u32[]{:S(2)}, u32[]{:S(2)}) collective-permute-start(f32[64,128]{1,0:T(8,128)S(1)} %get-tuple-element.40), channel_id=1, source_target_pairs={{1,2},{3,4},{5,6},{2,1},{4,3},{6,5},{9,10},{11,12},{13,14},{10,9},... | collective-permute-start | bytes 98312 | tf_op jit(solution)/shard_map/ppermute | solution.py:275
